TPU v7x, 512 devices: a whole 4x8x8 slice. The times are simulated.
512 devices in a mesh: row: 32 (over y, x), col: 16 (over z, core).
Axes of the slice: x: 4, y: 8, z: 8, core: 2. Of those that a mesh axis runs over, the one named last changes fastest.
Arguments:
- atom_types: int32 [512, 256], P(('row', 'col')), may hold values from 0 to 3
- neighbor_ids: int32 [512, 32, 256], P(('row', 'col')), may hold values from 0 to 255
- switching: float32 [512, 32, 256], P(('row', 'col')), may hold values from 0.1 to 1
- environment: float32 [512, 256, 64], P(('row', 'col')), may hold values from -6 to 6
- force_weights: float32 [512, 256], P(('row', 'col')), may hold values from -1 to 1
- targets: float32 [512], P(('row', 'col')), may hold values from -6 to 6
- type_embed: float32 [4, 64], replicated, may hold values from -8 to 8, as said below
- layer_weight: float32 [64, 128], replicated, may hold values from -1 to 1
- out_weight: float32 [128], replicated, may hold values from -0.5 to 0.5
- covariance: float32 [8192, 8192], P('row', 'col'), as said below
Outputs:
- new_weight: float32 [8192], P(('row', 'col'))
- new_cov: float32 [8192, 8192], P('row', 'col')
Inputs may be any that keep to these rules, and one draw needn't show every extreme that they name: `neighbor_ids`: indices of atoms of the same configuration. `covariance`: symmetric positive definite. `type_embed`: each feature sums to zero over the 4 types.
All inputs are finite; a program needn't handle non-finite values. Where the computation divides by a largest or mean magnitude, that divisor is 1e-20 or more.
Results may differ from a plain program's by a relative error of at most 0.0003.
Values sent between devices are 32-bit elements; how exact they have to be, the bound alone decides.
A program may use at most 64 MiB of HBM per device.

v0:
```python
import math

import jax
import jax.numpy as jnp
from jax import lax
from jax.sharding import PartitionSpec as P

NEWTON = 4


forget = 0.98
highest = lax.Precision.HIGHEST


def network(
    atom_types,
    neighbor_ids,
    switching,
    environment,
    force_weights,
    type_embed,
    layer_weight,
    out_weight,
):
    type_ids = jnp.arange(type_embed.shape[0], dtype=jnp.int32)
    onehot = (atom_types[:, None] == type_ids[None, :]).astype(jnp.float32)
    mixed = environment + jnp.dot(onehot, type_embed, precision=highest)
    nearby = jnp.take(mixed, neighbor_ids, axis=0)
    descriptor = jnp.sum(switching[:, :, None] * nearby, axis=0) / math.sqrt(neighbor_ids.shape[0])
    hidden = jnp.tanh(descriptor)
    activity = jnp.tanh(jnp.dot(hidden, layer_weight, precision=highest))
    energy = jnp.dot(activity, out_weight, precision=highest)
    atom_scale = 1.0 / math.sqrt(energy.shape[0])
    predicted = jnp.sum(force_weights * energy) * atom_scale
    slopes = out_weight[None, :] * (1.0 - activity * activity)
    jacobian = jnp.dot((force_weights[:, None] * hidden).T, slopes, precision=highest) * atom_scale
    return (predicted, jacobian.reshape(-1))


def contract_rows(left, right):
    return lax.dot_general(left, right, (((1,), (1,)), ((), ())), precision=highest)


def contract_first(left, right):
    return lax.dot_general(left, right, (((0,), (1,)), ((), ())), precision=highest)


def newton_rows(inverse, innovation, groups, position):
    height = inverse.shape[0] // groups
    window = lax.dynamic_slice_in_dim(inverse, position * height, height, 0)
    return 2.0 * window - jnp.dot(
        jnp.dot(window, innovation, precision=highest), inverse, precision=highest
    )


def on_device(
    atom_types,
    neighbor_ids,
    switching,
    environment,
    force_weights,
    targets,
    type_embed,
    layer_weight,
    out_weight,
    covariance,
):
    rows_n = lax.axis_size("row")
    cols_n = lax.axis_size("col")
    row_at = lax.axis_index("row")
    col_at = lax.axis_index("col")
    predicted, jacobian = jax.vmap(network, in_axes=(0, 0, 0, 0, 0, None, None, None))(
        atom_types,
        neighbor_ids,
        switching,
        environment,
        force_weights,
        type_embed,
        layer_weight,
        out_weight,
    )
    errors = targets - predicted
    per_dev = jacobian.shape[0]
    params = jacobian.shape[1]
    streams = per_dev * rows_n * cols_n
    slab_rows = params // (rows_n * cols_n)
    tile_rows = covariance.shape[0]
    blocks = jacobian.reshape(1, 1, per_dev, cols_n, rows_n, slab_rows)
    spread = jnp.broadcast_to(errors.reshape(1, 1, per_dev, 1, 1), (1, 1, per_dev, cols_n, rows_n))
    own_cols, all_errors = (
        lax.all_to_all(
            lax.all_to_all(blocks, "row", split_axis=4, concat_axis=0, tiled=True),
            "col",
            split_axis=3,
            concat_axis=1,
            tiled=True,
        ),
        lax.all_to_all(
            lax.all_to_all(spread, "row", split_axis=4, concat_axis=0, tiled=True),
            "col",
            split_axis=3,
            concat_axis=1,
            tiled=True,
        ),
    )
    own_cols = own_cols.reshape(streams, slab_rows)
    all_errors = all_errors.reshape(streams)
    row_pieces = jacobian.reshape(1, 1, per_dev, rows_n, tile_rows)
    row_pieces = lax.all_to_all(row_pieces, "row", split_axis=3, concat_axis=0, tiled=True)
    row_jac = lax.all_gather(row_pieces, "col", axis=1, tiled=True).reshape(streams, tile_rows)
    window = covariance
    rows_term = contract_rows(window, lax.all_gather(own_cols, "row", axis=1, tiled=True))
    window = covariance
    cross_own = lax.psum_scatter(
        contract_first(window, row_jac), "row", scatter_dimension=0, tiled=True
    )
    identity = jnp.eye(streams, dtype=jnp.float32)
    innovation = (
        lax.psum(jnp.dot(own_cols, cross_own, precision=highest), ("row", "col"))
        + forget * identity
    )
    row_bound = jnp.max(jnp.sum(jnp.abs(innovation), axis=1))
    inverse = identity * (2.0 / row_bound) - innovation / (row_bound * row_bound)
    for repeat in range(NEWTON - 1):
        inverse = lax.all_gather(
            newton_rows(inverse, innovation, cols_n, col_at), "col", axis=0, tiled=True
        )
    cross_rows = lax.psum(rows_term, "col")
    gain_rows = jnp.dot(cross_rows, inverse, precision=highest)
    gain_own = lax.dynamic_slice_in_dim(gain_rows, col_at * slab_rows, slab_rows, 0)
    flat_weight = layer_weight.reshape(-1)
    own_weight = lax.dynamic_slice_in_dim(
        flat_weight, (row_at * cols_n + col_at) * slab_rows, slab_rows, 0
    )
    new_weight = own_weight + jnp.dot(gain_own, all_errors, precision=highest)
    update = contract_rows(gain_rows, lax.all_gather(cross_own, "row", axis=0, tiled=True))
    new_cov = (covariance - update) / forget
    return (new_weight, new_cov)


def solution(mesh):
    in_specs = (
        P(("row", "col"), None),
        P(("row", "col"), None, None),
        P(("row", "col"), None, None),
        P(("row", "col"), None, None),
        P(("row", "col"), None),
        P(("row", "col")),
        P(),
        P(),
        P(),
        P("row", "col"),
    )
    out_specs = (P(("row", "col")), P("row", "col"))
    return jax.shard_map(
        on_device, mesh=mesh, in_specs=in_specs, out_specs=out_specs, check_vma=False
    )
```

profile of v0, /device:TPU:1, one launch (start us, length us, event | category | flops | bytes accessed | tf_op | source)
XLA Modules:
  0.0 1052.4 jit_solution(9687664694343574366)
XLA Ops:
  10.1 73.6 %gather_fusion = f32[8192,64]{1,0:T(8,128)} fusion(f32[1,256,64]{2,1,0:T(8,128)S(1)} %copy.15, s32[8192]{0:T(1024)S(1)} %bitcast.81), kind=kCustom, calls=%fused_computation | custom fusion | bytes 4259840 | tf_op jit(solution)/shard_map/vmap(jit(_take))/gather | solution.py:28
  83.7 6.1 multiply_reduce_fusion
  90.6 19.0 %all_to_all.66 = f32[1,1,1,32,256]{4,2,1,0,3:T(1,128)S(1)} all-to-all(f32[1,1,1,32,256]{4,2,1,0,3:T(1,128)S(1)} %bitcast.86), channel_id=1, replica_groups=mesh['row'=32,'col'=16] {'row'}, dimensions={3} | all-to-all | bytes 65536 | tf_op jit(solution)/shard_map/all_to_all | solution.py:109
  109.6 26.5 %all-gather = f32[1,1,1,32,4096]{4,2,1,0,3:T(1,128)S(1)} all-gather(f32[1,1,1,32,256]{4,2,1,0,3:T(1,128)S(1)} %all_to_all.66), channel_id=2, replica_groups=mesh['row'=32,'col'=16] {'col'}, dimensions={4}, use_global_device_ids=true | all-gather | bytes 557056 | tf_op jit(solution)/shard_map/all_gather | solution.py:110
  140.4 11.7 %all_to_all.67 = f32[32,1,256]{2,1,0:T(1,128)S(1)} all-to-all(f32[32,1,256]{2,1,0:T(1,128)S(1)} %reshape.157), channel_id=1, replica_groups=mesh['row'=32,'col'=16] {'row'}, dimensions={0} | all-to-all | bytes 65536 | tf_op jit(solution)/shard_map/all_to_all | solution.py:92
  153.8 11.1 %all_to_all.68 = f32[16,1,512]{2,1,0:T(1,128)S(1)} all-to-all(f32[16,1,512]{2,1,0:T(1,128)S(1)} %reshape.159), channel_id=1, replica_groups=mesh['row'=32,'col'=16] {'col'}, dimensions={0} | all-to-all | bytes 65536 | tf_op jit(solution)/shard_map/all_to_all | solution.py:91
  166.0 180.5 %reduce-scatter.4.cloned.1.call-done = f32[16,512]{1,0:T(8,128)} async-done(((f32[512,512]{1,0:T(8,128)}), f32[16,512]{1,0:T(8,128)}) %reduce-scatter.4.cloned.1.call-update) | async-done | bytes 32784
  346.5 2.8 fusion.40
  349.4 281.6 %all-reduce.5.cloned.1.call-done = f32[512,512]{1,0:T(8,128)} async-done(((f32[512,512]{1,0:T(8,128)}), f32[512,512]{1,0:T(8,128)}) %all-reduce.5.cloned.1.call-update) | async-done | bytes 1048592 | tf_op jit(solution)/shard_map/psum | solution.py:119
  636.4 1.9 fusion.6
  640.4 38.0 %all-gather.9.cloned.1.call-done = f32[512,512]{1,0:T(8,128)} async-done(((f32[32,512]{1,0:T(8,128)}), f32[512,512]{1,0:T(8,128)}) %all-gather.9.cloned.1.call-update) | async-done | bytes 1048592 | tf_op jit(solution)/shard_map/all_gather | solution.py:125
  680.0 2.6 convolution_subtract_fusion.2
  682.8 73.1 %all-gather.7.cloned.1.call-done = f32[512,512]{0,1:T(8,128)} async-done(((f32[512,16]{0,1:T(8,128)}), f32[512,512]{0,1:T(8,128)}) %all-gather.7.cloned.1.call-update) | async-done | bytes 1048592 | tf_op jit(solution)/shard_map/all_gather | solution.py:112
  755.9 3.8 convolution_bitcast_fusion.1
  759.8 43.1 %all-gather.11.cloned.1.call-done = f32[512,512]{1,0:T(8,128)} async-done(((f32[32,512]{1,0:T(8,128)}), f32[512,512]{1,0:T(8,128)}) %all-gather.11.cloned.1.call-update) | async-done | bytes 1048592 | tf_op jit(solution)/shard_map/all_gather | solution.py:125
  804.5 2.6 convolution_subtract_fusion.1
  810.0 17.7 %all_to_all.69 = f32[1,1,1,16,32]{3,2,1,0,4:T(1,128)S(1)} all-to-all(f32[1,1,1,16,32]{3,2,1,0,4:T(1,128)S(1)} %broadcast_in_dim.28), channel_id=1, replica_groups=mesh['row'=32,'col'=16] {'row'}, dimensions={4} | all-to-all | bytes 4096 | tf_op jit(solution)/shard_map/all_to_all | solution.py:99
  828.3 5.9 all-to-all-start.4
  834.2 7.0 all-to-all-done.4
  841.4 79.1 %all-reduce.3.cloned.1.call-done = f32[256,512]{0,1:T(8,128)} async-done(((f32[256,512]{0,1:T(8,128)}), f32[256,512]{0,1:T(8,128)}) %all-reduce.3.cloned.1.call-update) | async-done | bytes 524304 | tf_op jit(solution)/shard_map/psum | solution.py:128
  920.6 44.3 %all-gather.13.cloned.1.call-done = f32[512,512]{1,0:T(8,128)} async-done(((f32[32,512]{1,0:T(8,128)}), f32[512,512]{1,0:T(8,128)}) %all-gather.13.cloned.1.call-update) | async-done | bytes 1048592 | tf_op jit(solution)/shard_map/all_gather | solution.py:125
  964.8 2.4 fusion.41
  968.0 74.5 %all-gather.15.cloned.1.call-done = f32[512,512]{1,0:T(8,128)} async-done(((f32[16,512]{1,0:T(8,128)}), f32[512,512]{1,0:T(8,128)}) %all-gather.15.cloned.1.call-update) | async-done | bytes 1048592 | tf_op jit(solution)/shard_map/all_gather | solution.py:136
  1042.4 3.1 fusion
  (70 shorter events, 22.5 us)
Async XLA Ops:
  7.2 1.6 copy-start
  7.2 339.4 %reduce-scatter.4.cloned.1.call-start = ((), (), s32[]{:S(2)}) async-start(), calls=%async_computation.13 | async-start | bytes 1081344
  10.1 73.6 %copy-start.5 = (f32[1,32,256]{2,1,0:T(8,128)S(1)}, f32[1,32,256]{2,1,0:T(8,128)}, u32[]{:S(2)}) copy-start(f32[1,32,256]{2,1,0:T(8,128)} %param.12) | copy-start | bytes 98308
  83.7 6.2 copy-start.4
  83.7 6.5 copy-start.6
  83.7 6.5 copy-start.7
  83.7 53.8 %copy-start.2 = (f32[256,512]{1,0:T(8,128)S(1)}, f32[256,512]{1,0:T(8,128)}, u32[]{:S(2)}) copy-start(f32[256,512]{1,0:T(8,128)} %param.19) | copy-start | bytes 1572868
  139.9 491.1 %all-reduce.5.cloned.1.call-start = ((), (), s32[]{:S(2)}) async-start(), calls=%async_computation.8 | async-start | bytes 2097152 | tf_op jit(solution)/shard_map/psum | solution.py:119
  166.0 473.8 %copy-start.3 = (f32[512,16]{0,1:T(8,128)}, f32[512,16]{0,1:T(8,128)S(1)}, u32[]{:S(2)}) copy-start(f32[512,16]{0,1:T(8,128)S(1)} %reshape.134) | copy-start | bytes 98308
  349.3 329.1 %all-gather.9.cloned.1.call-start = ((), (), s32[]{:S(2)}) async-start(), calls=%async_computation.9 | async-start | bytes 1114112 | tf_op jit(solution)/shard_map/all_gather | solution.py:125
  631.0 47.5 %copy-start.1 = (f32[512,512]{1,0:T(8,128)S(1)}, f32[512,512]{1,0:T(8,128)}, u32[]{:S(2)}) copy-start(f32[512,512]{1,0:T(8,128)} %all-reduce.5.cloned.1.call-done) | copy-start | bytes 3145732
  639.8 116.2 %all-gather.7.cloned.1.call-start = ((), (), s32[]{:S(2)}) async-start(), calls=%async_computation.6 | async-start | bytes 1081344 | tf_op jit(solution)/shard_map/all_gather | solution.py:112
  640.4 162.6 %all-gather.11.cloned.1.call-start = ((), (), s32[]{:S(2)}) async-start(), calls=%async_computation.10 | async-start | bytes 1114112 | tf_op jit(solution)/shard_map/all_gather | solution.py:125
  682.6 237.9 %all-reduce.3.cloned.1.call-start = ((), (), s32[]{:S(2)}) async-start(), calls=%async_computation.7 | async-start | bytes 1048576 | tf_op jit(solution)/shard_map/psum | solution.py:128
  759.8 205.0 %all-gather.13.cloned.1.call-start = ((), (), s32[]{:S(2)}) async-start(), calls=%async_computation.11 | async-start | bytes 1114112 | tf_op jit(solution)/shard_map/all_gather | solution.py:125
  807.1 235.4 %all-gather.15.cloned.1.call-start = ((), (), s32[]{:S(2)}) async-start(), calls=%async_computation.12 | async-start | bytes 1081344 | tf_op jit(solution)/shard_map/all_gather | solution.py:136
  828.3 12.9 %all-to-all-start.4 = ((f32[32,1,1,16,1]{0,4,2,1,3:T(1,128)}), f32[32,1,1,16,1]{0,4,2,1,3:T(1,128)S(1)}, u32[]{:S(2)}, u32[]{:S(2)}) async-start(f32[32,1,1,16,1]{0,4,2,1,3:T(1,128)} %copy.20), calls=%async_computation.4 | async-start | bytes 16384 | tf_op jit(solution)/shard_map/all_to_all | solution.py:98
Sparse Core Ops, SparseCore 0:
  140.0 206.5 reduce-scatter.3
  351.6 279.3 all-reduce.4
  639.9 38.5 all-gather.8
  681.5 74.4 all-gather.6
  757.9 44.9 all-gather.10
  805.7 114.8 all-reduce.2
  922.7 42.0 all-gather.12
  968.0 74.4 all-gather.14
where the time goes:
time: 1060 us; the launch traced here: 1050 us
  waiting for transfers between devices  823 us (78%)
  blocking collectives  86 us (8%)
  local copies, waits for them, and re-layouts  77.7 us (7%)
  matrix products  28.1 us (3%)
  between operations  17.7 us (2%)
  other arithmetic  13.9 us (1%)
    psum x1, waiting for transfers between devices, on_device(): lax.psum(jnp.dot(own_cols, cross_own, precision=highest), ('row', 'col'))  282 us
    unnamed x9, waiting for transfers between devices  182 us
    all_gather x3, waiting for transfers between devices, on_device(): lax.all_gather(newton_rows(inverse, innovation, cols_n, col_at), 'col', a...  125 us
    psum x1, waiting for transfers between devices, on_device(): cross_rows = lax.psum(rows_term, 'col')  79.1 us
    all_gather x1, waiting for transfers between devices, on_device(): lax.all_gather(cross_own, 'row', axis=0, tiled=True)  74.5 us
    gather x2, local copies, waits for them, and re-layouts, network(): nearby = jnp.take(mixed, neighbor_ids, axis=0)  73.6 us
    all_gather x1, waiting for transfers between devices, on_device(): lax.all_gather(own_cols, 'row', axis=1, tiled=True)  73.1 us
    all_gather x1, blocking collectives, on_device(): lax.all_gather(row_pieces, 'col', axis=1, tiled=True)  26.5 us
  transfers between devices with their start and end apart: 9, of which 9 were waited for; matrix products, arithmetic and copies ran while one was open for 2% of the time, Pallas kernels for 0%

commit v1 on v0

v1 whole, which is shorter than its diff:
```python
import functools
import math

import jax
import jax.numpy as jnp
from jax import lax
from jax.experimental import pallas as pl
from jax.experimental.pallas import tpu as pltpu
from jax.sharding import PartitionSpec as P

FORGET = 0.98
MESH = pl.DeviceIdType.MESH
F32 = jnp.float32
BF16 = jnp.bfloat16
NX, NY, NZ = 4, 8, 8
NR, NC = 32, 16


def split(a):
    hi = a.astype(BF16)
    lo = (a - hi.astype(F32)).astype(BF16)
    return hi, lo


def mm(a, b, dims):
    return lax.dot_general(a, b, (dims, ((), ())), preferred_element_type=F32)


def dot3(a, b, dims):
    ah, al = a if isinstance(a, tuple) else split(a)
    bh, bl = b if isinstance(b, tuple) else split(b)
    return mm(ah, bh, dims) + (mm(ah, bl, dims) + mm(al, bh, dims))


ROWS = ((1,), (1,))
COLS = ((0,), (0,))
NORMAL = ((1,), (0,))


def kernel(
    types_ref, nbr_ref, sw_ref, env_ref, fw_ref, tgt_ref, te_ref, w_ref, ow_ref, cov_ref,
    newcov_ref, delta_ref,
    select, jrow_send, jcol_send, e_send, jr_recv, jc_recv, e_recv, e_all,
    jr_all, jc_all, w_send, w_recv, art,
    w2_send, x_recv, y_send, y_recv, act,
    s_send, s_recv, s_row, s_all,
    send, recv, jc_y, act_y, s_z,
):
    r = lax.axis_index("row")
    c = lax.axis_index("col")
    x, y = lax.rem(r, NX), lax.div(r, NX)
    k, z = lax.rem(c, 2), lax.div(c, 2)

    def row_peer(j):
        return lax.rem(r + j, NR)

    def col_peer(j):
        return lax.rem(c + j, NC)

    def x_peer(j):
        return y * NX + lax.rem(x + j, NX)

    def y_peer(j):
        return lax.rem(y + j, NY) * NX + x

    def z_peer(j):
        return lax.rem(z + j, NZ) * 2 + k

    def push(src, dst, send_sem, recv_sem, **where):
        pltpu.make_async_remote_copy(
            src_ref=src, dst_ref=dst, send_sem=send_sem, recv_sem=recv_sem,
            device_id=where, device_id_type=MESH,
        ).start()

    def settle(ref, sem):
        pltpu.make_async_copy(ref, ref, sem).wait()

    barrier = pltpu.get_barrier_semaphore()

    @pl.loop(1, NR)
    def _(j):
        pl.semaphore_signal(barrier, inc=1, device_id={"row": row_peer(j)}, device_id_type=MESH)

    @pl.loop(1, NC)
    def _(j):
        pl.semaphore_signal(barrier, inc=1, device_id={"col": col_peer(j)}, device_id_type=MESH)

    block = 32

    @pl.loop(0, 256 // block)
    def _(b):
        ids = lax.broadcasted_iota(jnp.int32, (block, 256), 0) + b * block
        total = jnp.zeros((block, 256), F32)
        for n in range(32):
            total += jnp.where(ids == nbr_ref[n : n + 1, :], sw_ref[n : n + 1, :], 0.0)
        select[pl.ds(b * block, block), :] = total

    kinds = lax.broadcasted_iota(jnp.int32, (4, 256), 0)
    onehot = (kinds == types_ref[...]).astype(F32)
    mixed = env_ref[...] + dot3(onehot, te_ref[...], COLS)
    descriptor = dot3(mixed, select[...], COLS) / math.sqrt(32)
    hidden = jnp.tanh(descriptor)
    activity = jnp.tanh(dot3(hidden, w_ref[...], COLS))
    weighted = dot3(fw_ref[...], activity, NORMAL)
    scale = 1.0 / math.sqrt(256)
    predicted = jnp.sum(weighted * ow_ref[...], axis=1, keepdims=True) * scale
    error = tgt_ref[...] - predicted
    slopes = ow_ref[...] * (1.0 - activity * activity)
    jac = dot3(hidden * fw_ref[...], slopes, NORMAL) * scale

    for n in range(NR):
        jrow_send[n] = jac[2 * n : 2 * n + 2, :]
    for n in range(NC):
        jcol_send[n] = jac[4 * n : 4 * n + 4, :]
    e_send[0] = jnp.broadcast_to(error, (1, 128))

    pl.semaphore_wait(barrier, NR - 1 + NC - 1)

    @pl.loop(1, NC)
    def _(j):
        p = col_peer(j)
        push(jcol_send.at[p], jc_recv.at[c], send.at[0], recv.at[0], col=p)

    @pl.loop(1, NR)
    def _(j):
        p = row_peer(j)
        push(jrow_send.at[p], jr_recv.at[r], send.at[1], recv.at[1], row=p)
        push(e_send.at[0], e_recv.at[r], send.at[2], recv.at[2], row=p)

    jc_recv[c] = jcol_send[c]
    jr_recv[r] = jrow_send[r]
    e_recv[r] = e_send[0]

    settle(jc_recv.at[pl.ds(0, NC - 1)], recv.at[0])
    jc_all[r] = jnp.concatenate([jc_recv[:, n, :] for n in range(4)], axis=1)

    def gather_y(buf, sem, first, sems):
        for j in (1, 7, 2, 6, 3, 5, 4):
            push(buf.at[r], buf.at[r], send.at[first], sems.at[j], row=y_peer(j))
        for i in (1, 3, 2):
            push(buf.at[r], buf.at[r], send.at[first + 1], recv.at[sem], row=x_peer(i))

    def gather_x(buf, sem, first, sems):
        for j in (1, 7, 2, 6, 3, 5, 4):
            slot = y_peer(NY - j)
            settle(buf.at[slot], sems.at[j])
            for i in (1, 3, 2):
                push(buf.at[slot], buf.at[slot], send.at[first + 1], recv.at[sem], row=x_peer(i))

    gather_y(jc_all, 3, 3, jc_y)

    settle(jr_recv.at[pl.ds(0, NR - 1)], recv.at[1])
    jr_all[c] = jnp.concatenate([jr_recv[:, n, :] for n in range(2)], axis=1)
    settle(e_recv.at[pl.ds(0, NR - 1)], recv.at[2])
    lanes = lax.broadcasted_iota(jnp.int32, (NR, 128), 1)
    spots = lax.broadcasted_iota(jnp.int32, (NR, 128), 0)
    e_all[c] = jnp.sum(jnp.where(lanes == spots, e_recv[:, 0, :], 0.0), axis=0, keepdims=True)

    @pl.loop(1, NC)
    def _(j):
        p = col_peer(j)
        push(jr_all.at[c], jr_all.at[c], send.at[5], recv.at[4], col=p)
        push(e_all.at[c], e_all.at[c], send.at[6], recv.at[5], col=p)

    gather_x(jc_all, 3, 3, jc_y)
    settle(jc_all.at[pl.ds(0, NX * NY - NY)], recv.at[3])

    cov = split(cov_ref[...])
    part = dot3(jc_all[...].reshape(512, 512), cov, ROWS)
    at = lax.broadcasted_iota(jnp.int32, (512, 512), 0)
    to = lax.broadcasted_iota(jnp.int32, (512, 512), 1)
    order = (to == lax.rem(at, NR) * NC + lax.div(at, NR)).astype(F32).astype(BF16)
    ph, plow = split(part)
    part = mm(order, ph, NORMAL) + mm(order, plow, NORMAL)
    w_send[...] = part.reshape(NC, NR, 256)

    @pl.loop(1, NC)
    def _(j):
        p = col_peer(j)
        push(w_send.at[p], w_recv.at[c], send.at[7], recv.at[6], col=p)

    w_recv[c] = w_send[c]

    settle(jr_all.at[pl.ds(0, NC - 1)], recv.at[4])
    jr = split(jr_all[...].reshape(512, 256))
    w2_send[...] = dot3(jr, cov, NORMAL).reshape(NY, NX, 16, 512)
    for i in (1, 3, 2):
        px = lax.rem(x + i, NX)
        push(w2_send.at[:, px], x_recv.at[i], send.at[8], recv.at[7], row=x_peer(i))

    settle(w_recv.at[pl.ds(0, NC - 1)], recv.at[6])
    own = jnp.sum(w_recv[...], axis=0)
    art[c] = own
    s_part = dot3(own, jr, ROWS)
    for n in range(4):
        s_send[:, n, :] = s_part[:, 128 * n : 128 * n + 128]

    @pl.loop(1, NR)
    def _(j):
        p = row_peer(j)
        push(s_send.at[p], s_recv.at[r], send.at[9], recv.at[8], row=p)

    s_recv[r] = s_send[r]

    @pl.loop(1, NC)
    def _(j):
        push(art.at[c], art.at[c], send.at[10], recv.at[9], col=col_peer(j))

    settle(s_recv.at[pl.ds(0, NR - 1)], recv.at[8])
    s_row[r] = jnp.sum(s_recv[...], axis=0)

    @pl.loop(1, NR)
    def _(j):
        push(s_row.at[r], s_row.at[r], send.at[11], recv.at[10], row=row_peer(j))

    settle(x_recv.at[pl.ds(1, NX - 1)], recv.at[7])
    y_send[...] = w2_send[:, x] + x_recv[1] + x_recv[2] + x_recv[3]
    for j in (1, 7, 2, 6, 3, 5, 4):
        py = lax.rem(y + j, NY)
        push(y_send.at[py], y_recv.at[j], send.at[12], recv.at[11], row=y_peer(j))

    settle(s_row.at[pl.ds(0, NR - 1)], recv.at[10])
    s_all[c] = jnp.concatenate([s_row[:, n, :] for n in range(4)], axis=1)
    for j in (1, 7, 2, 6, 3, 5, 4):
        push(s_all.at[c], s_all.at[c], send.at[13], s_z.at[j], col=z_peer(j))
    partner = z * 2 + 1 - k
    push(s_all.at[c], s_all.at[c], send.at[14], recv.at[12], col=partner)

    settle(y_recv.at[pl.ds(1, NY - 1)], recv.at[11])
    total = y_send[y]
    for j in range(1, NY):
        total += y_recv[j]
    act[r] = total
    gather_y(act, 13, 15, act_y)

    for j in (1, 7, 2, 6, 3, 5, 4):
        slot = z_peer(NZ - j)
        settle(s_all.at[slot], s_z.at[j])
        push(s_all.at[slot], s_all.at[slot], send.at[14], recv.at[12], col=partner)
    gather_x(act, 13, 15, act_y)
    settle(s_all.at[pl.ds(0, NZ)], recv.at[12])

    eye = at == to
    innovation = s_all[...].reshape(512, 512) + jnp.where(eye, FORGET, 0.0)
    bound = jnp.max(jnp.sum(jnp.abs(innovation), axis=0, keepdims=True), axis=1, keepdims=True)
    settle(art.at[pl.ds(0, NC - 1)], recv.at[9])
    power = split(jnp.where(eye, 1.0, 0.0) - innovation / bound)
    gain = art[...].reshape(512, 256) / bound
    for step in range(4):
        gain = gain + dot3(power, gain, NORMAL)
        if step < 3:
            power = split(dot3(power, power, NORMAL))

    settle(e_all.at[pl.ds(0, NC - 1)], recv.at[5])
    spread = (
        lax.broadcasted_iota(jnp.int32, (512, NC), 1)
        == lax.div(lax.broadcasted_iota(jnp.int32, (512, NC), 0), NR)
    ).astype(F32)
    errors = jnp.concatenate([e_all[n] for n in range(NC)], axis=0)
    picked = jnp.dot(spread, errors, precision=lax.Precision.HIGHEST)
    own_lane = lax.broadcasted_iota(jnp.int32, (512, 128), 1) == lax.rem(
        lax.broadcasted_iota(jnp.int32, (512, 128), 0), NR
    )
    column = jnp.sum(jnp.where(own_lane, picked, 0.0), axis=1, keepdims=True)
    delta_ref[...] = jnp.sum(gain * column, axis=0, keepdims=True)

    settle(act.at[pl.ds(0, NX * NY - NY)], recv.at[13])
    update = dot3(gain, act[...].reshape(512, 512), COLS)
    newcov_ref[...] = (cov_ref[...] - update) * (1.0 / FORGET)

    settle(jcol_send.at[pl.ds(0, NC - 1)], send.at[0])
    settle(jrow_send.at[pl.ds(0, NR - 1)], send.at[1])
    settle(e_recv.at[pl.ds(0, NR - 1)], send.at[2])
    settle(jc_all.at[pl.ds(0, NY - 1)], send.at[3])
    settle(jc_all.at[pl.ds(0, NX * NY - NY)], send.at[4])
    settle(jr_all.at[pl.ds(0, NC - 1)], send.at[5])
    settle(e_all.at[pl.ds(0, NC - 1)], send.at[6])
    settle(w_send.at[pl.ds(0, NC - 1)], send.at[7])
    settle(x_recv.at[pl.ds(1, NX - 1)], send.at[8])
    settle(s_send.at[pl.ds(0, NR - 1)], send.at[9])
    settle(art.at[pl.ds(0, NC - 1)], send.at[10])
    settle(s_row.at[pl.ds(0, NR - 1)], send.at[11])
    settle(y_recv.at[pl.ds(1, NY - 1)], send.at[12])
    settle(s_all.at[pl.ds(0, NZ - 1)], send.at[13])
    settle(s_all.at[pl.ds(0, NZ)], send.at[14])
    settle(act.at[pl.ds(0, NY - 1)], send.at[15])
    settle(act.at[pl.ds(0, NX * NY - NY)], send.at[16])


def on_device(
    atom_types, neighbor_ids, switching, environment, force_weights, targets,
    type_embed, layer_weight, out_weight, covariance,
):
    vmem = pl.BlockSpec(memory_space=pltpu.VMEM)
    V = pltpu.VMEM
    scratch = [
        V((256, 256), F32), V((NR, 2, 128), F32), V((NC, 4, 128), F32), V((1, 1, 128), F32),
        V((NR, 2, 128), F32), V((NC, 4, 128), F32), V((NR, 1, 128), F32), V((NC, 1, 128), F32),
        V((NC, NR, 256), F32), V((NR, NC, 512), F32), V((NC, NR, 256), F32),
        V((NC, NR, 256), F32), V((NC, NR, 256), F32),
        V((NY, NX, 16, 512), F32), V((NX, NY, 16, 512), F32), V((NY, 16, 512), F32),
        V((NY, 16, 512), F32), V((NR, 16, 512), F32),
        V((NR, 4, 128), F32), V((NR, 4, 128), F32), V((NR, 4, 128), F32), V((NC, NR, 512), F32),
        pltpu.SemaphoreType.DMA((17,)), pltpu.SemaphoreType.DMA((14,)),
        pltpu.SemaphoreType.DMA((NY,)), pltpu.SemaphoreType.DMA((NY,)), pltpu.SemaphoreType.DMA((NZ,)),
    ]
    new_cov, delta = pl.pallas_call(
        kernel,
        out_shape=(
            jax.ShapeDtypeStruct((256, 512), F32),
            jax.ShapeDtypeStruct((1, 256), F32),
        ),
        in_specs=[vmem] * 10,
        out_specs=(vmem, vmem),
        scratch_shapes=scratch,
        compiler_params=pltpu.CompilerParams(
            collective_id=0, has_side_effects=True, vmem_limit_bytes=60 * 1024 * 1024
        ),
    )(
        atom_types, neighbor_ids[0], switching[0], environment[0], force_weights,
        targets.reshape(1, 1), type_embed, layer_weight, out_weight.reshape(1, 128), covariance,
    )
    row_at = lax.axis_index("row")
    col_at = lax.axis_index("col")
    flat_weight = layer_weight.reshape(-1)
    own_weight = lax.dynamic_slice_in_dim(flat_weight, (row_at * NC + col_at) * 16, 16, 0)
    new_weight = own_weight + lax.dynamic_slice_in_dim(delta[0], col_at * 16, 16, 0)
    return (new_weight, new_cov)


def solution(mesh):
    in_specs = (
        P(("row", "col"), None),
        P(("row", "col"), None, None),
        P(("row", "col"), None, None),
        P(("row", "col"), None, None),
        P(("row", "col"), None),
        P(("row", "col")),
        P(),
        P(),
        P(),
        P("row", "col"),
    )
    out_specs = (P(("row", "col")), P("row", "col"))
    return jax.shard_map(
        on_device, mesh=mesh, in_specs=in_specs, out_specs=out_specs, check_vma=False
    )
```

time: 1060 us -> 96.8 us (0.09)
  the two profiles are of different devices: /device:TPU:1 before, /device:TPU:40 now
where the time goes in v1:
time: 96.8 us; the launch traced here: 96.5 us
  Pallas kernels  89.8 us (93%)
  local copies, waits for them, and re-layouts  4.13 us (4%)
  between operations  1.3 us (1%)
  other arithmetic  1.27 us (1%)
    pallas_call x1, Pallas kernels, on_device(): pl.pallas_call(kernel, out_shape=(jax.ShapeDtypeStruct((256, 512), F32),...  89.8 us
    unnamed x4, local copies, waits for them, and re-layouts  4.13 us

profile of v1, /device:TPU:40, one launch (start us, length us, event | category | flops | bytes accessed | tf_op | source)
XLA Modules:
  0.0 96.5 jit_solution(4750589351745538860)
XLA Ops:
  1.3 1.6 %copy.12 = f32[1,256,64]{2,1,0:T(8,128)} copy(f32[1,256,64]{1,2,0:T(8,128)} %param.13) | data formatting | bytes 131072 | tf_op args[3]
  2.9 89.8 %shard_map.113 = (f32[256,512]{1,0:T(8,128)}, f32[1,256]{1,0:T(1,128)}) custom-call(s32[1,256]{1,0:T(1,128)} %types_ref.1, s32[32,256]{1,0:T(8,128)} %bitcast.11, f32[32,256]{1,0:T(8,128)} %bitcast.12, f32[256,64]{1,0:T(8,128)} %bitcast.9, f32[1,256]{1,0:T(1,128)} %fw_ref.1, f32[1,1]{1,0:T(1,128)} %bitcast.8.tgt_ref, f32[4,64]{1,0:T(4,128)} %te_ref.1, ...), custom_call_target="tpu_custom_call" | custom-call | tf_op jit(solution)/shard_map/pallas_call | solution.py:307
  92.7 0.0 copy-start
  92.7 0.7 copy-done
  93.4 1.3 %bitcast_add_fusion = f32[16]{0:T(128)} fusion(f32[1,256]{1,0:T(1,128)S(1)} %copy-done, s32[]{:T(128)S(6)} %select_n.7, f32[8192]{0:T(1024)} %bitcast.10, s32[]{:T(128)S(6)} %select_n.6), kind=kLoop, calls=%fused_computation | loop fusion | flops 16 | bytes 200 | tf_op jit(solution)/shard_map/add | solution.py:327
  94.7 1.9 %copy.15 = f32[256,512]{1,0:T(8,128)} copy(f32[256,512]{1,0:T(8,128)} %get-tuple-element.9) | data formatting | bytes 1048576
Async XLA Ops:
  92.7 0.7 copy-start

commit v2 on v1

v2 whole, which is shorter than its diff:
```python
import functools
import math

import jax
import jax.numpy as jnp
from jax import lax
from jax.experimental import pallas as pl
from jax.experimental.pallas import tpu as pltpu
from jax.sharding import PartitionSpec as P

FORGET = 0.98
MESH = pl.DeviceIdType.MESH
F32 = jnp.float32
BF16 = jnp.bfloat16
NX, NY, NZ = 4, 8, 8
NR, NC = 32, 16
NEAR = (1, 7, 2, 6, 3, 5, 4)
GROUPS = (
    "jcol", "jrow", "err", "jc_y", "jc_x", "jr_z", "jr_p", "e", "w", "art_z", "art_p",
    "s_x", "s_y", "s_z", "s_g", "s_p", "act_y", "act_x",
)


def split(a):
    hi = a.astype(BF16)
    lo = (a - hi.astype(F32)).astype(BF16)
    return hi, lo


def mm(a, b, dims):
    return lax.dot_general(a, b, (dims, ((), ())), preferred_element_type=F32)


def dot3(a, b, dims):
    ah, al = a if isinstance(a, tuple) else split(a)
    bh, bl = b if isinstance(b, tuple) else split(b)
    return mm(ah, bh, dims) + (mm(ah, bl, dims) + mm(al, bh, dims))


ROWS = ((1,), (1,))
COLS = ((0,), (0,))
NORMAL = ((1,), (0,))


def kernel(
    types_ref, nbr_ref, sw_ref, env_ref, fw_ref, tgt_ref, te_ref, w_ref, ow_ref, cov_ref,
    newcov_ref, weight_ref,
    select, cov_hi, cov_lo, order, jrow_send, jcol_send, e_send, jr_recv, jc_recv, e_recv, e_all,
    jr_all, jc_all, w_send, w_recv, art, turned, act,
    s_send, s_x, s_y, s_all,
    send, recv, jc_y, jc_x, act_y, s_z, s_g, turn_send, turn_recv,
):
    r = lax.axis_index("row")
    c = lax.axis_index("col")
    x, y = lax.rem(r, NX), lax.div(r, NX)
    k, z = lax.rem(c, 2), lax.div(c, 2)

    def row_peer(j):
        return lax.rem(r + j, NR)

    def col_peer(j):
        return lax.rem(c + j, NC)

    def x_peer(j):
        return y * NX + lax.rem(x + j, NX)

    def y_peer(j):
        return lax.rem(y + j, NY) * NX + x

    def z_peer(j):
        return lax.rem(z + j, NZ) * 2 + k

    partner = z * 2 + 1 - k
    flight = {}

    def push(name, src, dst, sem=None, **where):
        at = GROUPS.index(name)
        pltpu.make_async_remote_copy(
            src_ref=src, dst_ref=dst, send_sem=send.at[at],
            recv_sem=recv.at[at] if sem is None else sem,
            device_id=where, device_id_type=MESH,
        ).start()

    def settle(ref, sem):
        pltpu.make_async_copy(ref, ref, sem).wait()

    def track(name, sent, got=None):
        at = GROUPS.index(name)
        flight[name] = [(sent, send.at[at])]
        if got is not None:
            flight[name].append((got, recv.at[at]))

    def land(name):
        settle(*flight[name].pop())

    def drain():
        for waits in flight.values():
            for ref, sem in waits:
                settle(ref, sem)

    barrier = pltpu.get_barrier_semaphore()

    @pl.loop(1, NR)
    def _(j):
        pl.semaphore_signal(barrier, inc=1, device_id={"row": row_peer(j)}, device_id_type=MESH)

    @pl.loop(1, NC)
    def _(j):
        pl.semaphore_signal(barrier, inc=1, device_id={"col": col_peer(j)}, device_id_type=MESH)

    across = lax.div(r, 2)
    for h in range(2):

        @pl.when(2 * c + h != r)
        def _():
            pl.semaphore_signal(
                barrier, inc=1, device_id={"row": 2 * c + h, "col": across}, device_id_type=MESH
            )

    block = 32

    @pl.loop(0, 256 // block)
    def _(b):
        ids = lax.broadcasted_iota(jnp.int32, (block, 256), 0) + b * block
        total = jnp.zeros((block, 256), F32)
        for n in range(32):
            total += jnp.where(ids == nbr_ref[n : n + 1, :], sw_ref[n : n + 1, :], 0.0)
        select[pl.ds(b * block, block), :] = total

    kinds = lax.broadcasted_iota(jnp.int32, (4, 256), 0)
    onehot = (kinds == types_ref[...]).astype(F32)
    mixed = env_ref[...] + dot3(te_ref[...], onehot, COLS)
    descriptor = dot3(mixed, select[...], NORMAL) / math.sqrt(32)
    hidden = jnp.tanh(descriptor)
    activity = jnp.tanh(dot3(hidden, w_ref[...], COLS))
    weighted = dot3(fw_ref[...], activity, NORMAL)
    scale = 1.0 / math.sqrt(256)
    predicted = jnp.sum(weighted * ow_ref[...], axis=1, keepdims=True) * scale
    error = tgt_ref[...] - predicted
    slopes = ow_ref[...] * (1.0 - activity * activity)
    jac = dot3(hidden * fw_ref[...], slopes, NORMAL) * scale

    for n in range(NC):
        jcol_send[n] = jac[4 * n : 4 * n + 4, :]
    for n in range(NR):
        jrow_send[n] = jac[2 * n : 2 * n + 2, :]
    e_send[0] = jnp.broadcast_to(error, (1, 128))
    cov_hi[...], cov_lo[...] = split(cov_ref[...])
    at = lax.broadcasted_iota(jnp.int32, (512, 512), 0)
    to = lax.broadcasted_iota(jnp.int32, (512, 512), 1)
    order[...] = (to == lax.rem(at, NC) * NR + lax.div(at, NC)).astype(F32).astype(BF16)

    mirror = lax.div(r, 2) == c
    pl.semaphore_wait(barrier, NR - 1 + NC - 1 + 2 - mirror.astype(jnp.int32))

    @pl.loop(1, NC)
    def _(j):
        p = col_peer(j)
        push("jcol", jcol_send.at[p], jc_recv.at[c], col=p)

    @pl.loop(1, NR)
    def _(j):
        p = row_peer(j)
        push("jrow", jrow_send.at[p], jr_recv.at[r], row=p)

    @pl.loop(1, NC)
    def _(j):
        push("err", e_send.at[0], e_recv.at[c], col=col_peer(j))

    track("jcol", jcol_send.at[pl.ds(0, NC - 1)], jc_recv.at[pl.ds(0, NC - 1)])
    track("jrow", jrow_send.at[pl.ds(0, NR - 1)], jr_recv.at[pl.ds(0, NR - 1)])
    track("err", e_recv.at[pl.ds(0, NC - 1)], e_recv.at[pl.ds(0, NC - 1)])
    jc_recv[c] = jcol_send[c]
    jr_recv[r] = jrow_send[r]
    e_recv[c] = e_send[0]

    land("jcol")
    jc_all[r] = jnp.concatenate([jc_recv[:, n, :] for n in range(4)], axis=1)

    for j in NEAR:
        push("jc_y", jc_all.at[r], jc_all.at[r], jc_y.at[j], row=y_peer(j))
    for i in (1, 3, 2):
        push("jc_x", jc_all.at[r], jc_all.at[r], jc_x.at[0], row=x_peer(i))
    track("jc_y", jc_all.at[pl.ds(0, NY - 1)])
    track("jc_x", jc_all.at[pl.ds(0, NR - NY)])

    land("jrow")
    jr_all[z, k] = jnp.concatenate([jr_recv[:, n, :] for n in range(2)], axis=1)
    for j in NEAR:
        push("jr_z", jr_all.at[z, k], jr_all.at[z, k], col=z_peer(j))
    track("jr_z", jr_all.at[pl.ds(0, NZ - 1), 0], jr_all.at[pl.ds(0, NZ - 1), 0])

    def pass_jc(j):
        slot = y_peer(NY - j)
        settle(jc_all.at[slot], jc_y.at[j])
        for i in (1, 3, 2):
            push("jc_x", jc_all.at[slot], jc_all.at[slot], jc_x.at[j], row=x_peer(i))

    cov = (cov_hi[...], cov_lo[...])
    for j in NEAR[:3]:
        pass_jc(j)
    for n, j in enumerate((0,) + NEAR):
        there = lax.rem(y + NY - j, NY)
        settle(jc_all.at[pl.ds(0, NX - 1)], jc_x.at[j])
        part = dot3(jc_all[pl.ds(there * NX, NX)].reshape(64, 512), cov, ROWS)
        w_send[there] = part.reshape(2, NR, 256)
        for h in range(2):

            @pl.when(2 * there + h != c)
            def _():
                push("w", w_send.at[there, h], w_recv.at[c], col=2 * there + h)

            @pl.when(2 * there + h == c)
            def _():
                w_recv[c] = w_send[there, h]

        if n + 3 < len(NEAR):
            pass_jc(NEAR[n + 3])
        if n == 5:
            land("jr_z")
            push("jr_p", jr_all.at[:, k], jr_all.at[:, k], col=partner)
            track("jr_p", jr_all.at[:, 0], jr_all.at[:, 0])
    track("w", w_recv.at[pl.ds(0, NC - 1)], w_recv.at[pl.ds(0, NC - 1)])

    land("err")
    lanes = lax.broadcasted_iota(jnp.int32, (NC, 128), 1)
    spots = lax.broadcasted_iota(jnp.int32, (NC, 128), 0)
    e_all[r] = jnp.sum(jnp.where(lanes == spots, e_recv[:, 0, :], 0.0), axis=0, keepdims=True)

    land("jr_p")
    jh, jl = split(jr_all[...].reshape(512, 256))
    perm = order[...]
    jr = (mm(perm, jh, NORMAL).astype(BF16), mm(perm, jl, NORMAL).astype(BF16))

    land("w")
    own = jnp.sum(w_recv[...], axis=0)
    art[z, k] = own

    for h in range(2):

        @pl.when(2 * c + h != r)
        def _():
            pltpu.make_async_remote_copy(
                src_ref=art.at[z, k, pl.ds(16 * h, 16)], dst_ref=turned.at[lax.rem(r, 2)],
                send_sem=turn_send.at[h], recv_sem=turn_recv.at[lax.rem(r, 2)],
                device_id={"row": 2 * c + h, "col": across}, device_id_type=MESH,
            ).start()

        @pl.when(2 * c + h == r)
        def _():
            turned[h] = own[16 * h : 16 * h + 16, :]

    s_part = dot3(own, jr, ROWS)
    for n in range(NX):
        s_send[n] = s_part[8 * n : 8 * n + 8, :]
    for i in (1, 3, 2):
        push("s_x", s_send.at[lax.rem(x + i, NX)], s_x.at[x], row=x_peer(i))
    track("s_x", s_x.at[pl.ds(0, NX - 1)], s_x.at[pl.ds(0, NX - 1)])
    s_x[x] = s_send[x]

    for j in NEAR:
        push("art_z", art.at[z, k], art.at[z, k], col=z_peer(j))
    track("art_z", art.at[pl.ds(0, NZ - 1), 0], art.at[pl.ds(0, NZ - 1), 0])

    land("s_x")
    s_y[y] = jnp.sum(s_x[...], axis=0)
    for j in NEAR:
        push("s_y", s_y.at[y], s_y.at[y], row=y_peer(j))
    track("s_y", s_y.at[pl.ds(0, NY - 1)], s_y.at[pl.ds(0, NY - 1)])

    for h in range(2):

        @pl.when(2 * c + h != r)
        def _():
            settle(turned.at[h], turn_recv.at[h])
            settle(turned.at[h], turn_send.at[h])

    act[r] = jnp.concatenate([turned[0], turned[1]], axis=1)
    for j in NEAR:
        push("act_y", act.at[r], act.at[r], act_y.at[j], row=y_peer(j))
    for i in (1, 3, 2):
        push("act_x", act.at[r], act.at[r], row=x_peer(i))
    track("act_y", act.at[pl.ds(0, NY - 1)])

    land("s_y")
    mine = c * NX + x
    s_all[mine] = jnp.sum(s_y[...], axis=0)
    for j in NEAR:
        push("s_z", s_all.at[mine], s_all.at[mine], s_z.at[j], col=z_peer(j))
    for i in (1, 3, 2):
        push("s_g", s_all.at[mine], s_all.at[mine], s_g.at[0], row=x_peer(i))
    track("s_z", s_all.at[pl.ds(0, NZ - 1)])

    land("art_z")
    push("art_p", art.at[:, k], art.at[:, k], col=partner)
    track("art_p", art.at[:, 0], art.at[:, 0])

    @pl.loop(1, NR)
    def _(j):
        push("e", e_all.at[r], e_all.at[r], row=row_peer(j))

    track("e", e_all.at[pl.ds(0, NR - 1)], e_all.at[pl.ds(0, NR - 1)])

    for j in NEAR:
        slot = z_peer(NZ - j) * NX + x
        settle(s_all.at[slot], s_z.at[j])
        for i in (1, 3, 2):
            push("s_g", s_all.at[slot], s_all.at[slot], s_g.at[j], row=x_peer(i))
        slot = y_peer(NY - j)
        settle(act.at[slot], act_y.at[j])
        for i in (1, 3, 2):
            push("act_x", act.at[slot], act.at[slot], row=x_peer(i))
    track("s_g", s_all.at[pl.ds(0, NX * NZ - NZ)])
    track("act_x", act.at[pl.ds(0, NR - NY)], act.at[pl.ds(0, NR - NY)])
    for j in (0,) + NEAR:
        settle(s_all.at[pl.ds(0, NX - 1)], s_g.at[j])
        group = pl.ds(z_peer(NZ - j) * NX, NX)
        push("s_p", s_all.at[group], s_all.at[group], col=partner)
    track("s_p", s_all.at[pl.ds(0, NX * NZ)], s_all.at[pl.ds(0, NX * NZ)])
    land("s_p")

    eye = at == to
    innovation = s_all[...].reshape(512, 512) + jnp.where(eye, FORGET, 0.0)
    bound = jnp.max(jnp.sum(jnp.abs(innovation), axis=0, keepdims=True), axis=1, keepdims=True)
    land("art_p")
    power = split(jnp.where(eye, 1.0, 0.0) - innovation / bound)
    gain = art[...].reshape(512, 256) / bound
    for step in range(4):
        gain = gain + dot3(power, gain, NORMAL)
        if step < 3:
            power = split(dot3(power, power, NORMAL))

    land("e")
    spread = (
        lax.broadcasted_iota(jnp.int32, (512, NR), 1)
        == lax.div(lax.broadcasted_iota(jnp.int32, (512, NR), 0), NC)
    ).astype(F32)
    errors = jnp.concatenate([e_all[n] for n in range(NR)], axis=0)
    picked = jnp.dot(spread, errors, precision=lax.Precision.HIGHEST)
    own_lane = lax.broadcasted_iota(jnp.int32, (512, 128), 1) == lax.rem(
        lax.broadcasted_iota(jnp.int32, (512, 128), 0), NC
    )
    column = jnp.sum(jnp.where(own_lane, picked, 0.0), axis=1, keepdims=True)
    delta = jnp.sum(gain * column, axis=0, keepdims=True)
    half = lax.div(c, 8)
    delta = jnp.where(half == 0, delta[:, :128], delta[:, 128:])
    moved = w_ref[pl.ds(2 * r + half, 1), :] + delta
    moved = pltpu.roll(moved, 128 - 16 * lax.rem(c, 8), 1)
    weight_ref[...] = moved[:, :16]

    land("act_x")
    update = dot3(gain, act[...].reshape(512, 512), COLS)
    newcov_ref[...] = (cov_ref[...] - update) * (1.0 / FORGET)
    drain()


def on_device(
    atom_types, neighbor_ids, switching, environment, force_weights, targets,
    type_embed, layer_weight, out_weight, covariance,
):
    vmem = pl.BlockSpec(memory_space=pltpu.VMEM)
    V = pltpu.VMEM
    D = pltpu.SemaphoreType.DMA
    scratch = [
        V((256, 256), F32), V((256, 512), BF16), V((256, 512), BF16), V((512, 512), BF16),
        V((NR, 2, 128), F32), V((NC, 4, 128), F32), V((1, 1, 128), F32),
        V((NR, 2, 128), F32), V((NC, 4, 128), F32), V((NC, 1, 128), F32), V((NR, 1, 128), F32),
        V((NZ, 2, NR, 256), F32), V((NR, NC, 512), F32),
        V((NY, 2, NR, 256), F32), V((NC, NR, 256), F32), V((NZ, 2, NR, 256), F32),
        V((2, 16, 256), F32), V((NR, 16, 512), F32),
        V((NX, 8, 512), F32), V((NX, 8, 512), F32), V((NY, 8, 512), F32), V((NC * NX, 8, 512), F32),
        D((len(GROUPS),)), D((len(GROUPS),)), D((NY,)), D((NY,)), D((NY,)), D((NZ,)), D((NZ,)),
        D((2,)), D((2,)),
    ]
    new_cov, weight = pl.pallas_call(
        kernel,
        out_shape=(
            jax.ShapeDtypeStruct((256, 512), F32),
            jax.ShapeDtypeStruct((1, 16), F32),
        ),
        in_specs=[vmem] * 10,
        out_specs=(vmem, vmem),
        scratch_shapes=scratch,
        compiler_params=pltpu.CompilerParams(
            collective_id=0, has_side_effects=True, vmem_limit_bytes=60 * 1024 * 1024
        ),
    )(
        atom_types, neighbor_ids[0], switching[0], environment[0].T, force_weights,
        targets.reshape(1, 1), type_embed, layer_weight, out_weight.reshape(1, 128), covariance,
    )
    return (weight.reshape(16), new_cov)


def solution(mesh):
    in_specs = (
        P(("row", "col"), None),
        P(("row", "col"), None, None),
        P(("row", "col"), None, None),
        P(("row", "col"), None, None),
        P(("row", "col"), None),
        P(("row", "col")),
        P(),
        P(),
        P(),
        P("row", "col"),
    )
    out_specs = (P(("row", "col")), P("row", "col"))
    return jax.shard_map(
        on_device, mesh=mesh, in_specs=in_specs, out_specs=out_specs, check_vma=False
    )
```

time: 96.8 us -> 95.7 us (0.989)
  the two profiles are of different devices: /device:TPU:40 before, /device:TPU:1 now
where the time goes in v2:
time: 95.7 us; the launch traced here: 95.5 us
  Pallas kernels  91.2 us (95%)
  local copies, waits for them, and re-layouts  3.04 us (3%)
  between operations  1.3 us (1%)
    pallas_call x1, Pallas kernels, on_device(): pl.pallas_call(kernel, out_shape=(jax.ShapeDtypeStruct((256, 512), F32),...  91.2 us
    unnamed x4, local copies, waits for them, and re-layouts  3.04 us

profile of v2, /device:TPU:1, one launch (start us, length us, event | category | flops | bytes accessed | tf_op | source)
XLA Modules:
  0.0 95.5 jit_solution(14635422635029183801)
XLA Ops:
  1.3 91.2 %shard_map.113 = (f32[256,512]{1,0:T(8,128)}, f32[1,16]{1,0:T(1,128)}) custom-call(s32[1,256]{1,0:T(1,128)} %types_ref.1, s32[32,256]{1,0:T(8,128)} %bitcast.10, f32[32,256]{1,0:T(8,128)} %bitcast.11, f32[64,256]{1,0:T(8,128)} %bitcast.9, f32[1,256]{1,0:T(1,128)} %fw_ref.1, f32[1,1]{1,0:T(1,128)} %bitcast.8.tgt_ref, f32[4,64]{1,0:T(4,128)} %te_ref.1, ...), custom_call_target="tpu_custom_call" | custom-call | tf_op jit(solution)/shard_map/pallas_call | solution.py:375
  92.4 0.0 copy-start
  92.4 0.7 copy-done
  93.1 0.5 copy.15
  93.6 1.9 %copy.16 = f32[256,512]{1,0:T(8,128)} copy(f32[256,512]{1,0:T(8,128)} %get-tuple-element.9) | data formatting | bytes 1048576
Async XLA Ops:
  92.4 0.7 copy-start

commit v3 on v2

--- a/solution.py
+++ b/solution.py
@@ -17,7 +17,7 @@
 NEAR = (1, 7, 2, 6, 3, 5, 4)
 GROUPS = (
     "jcol", "jrow", "err", "jc_y", "jc_x", "jr_z", "jr_p", "e", "w", "art_z", "art_p",
-    "s_x", "s_y", "s_z", "s_g", "s_p", "act_y", "act_x",
+    "s", "s_yz", "s_x", "s_p", "act", "act_x",
 )
 
 
@@ -46,9 +46,9 @@
     types_ref, nbr_ref, sw_ref, env_ref, fw_ref, tgt_ref, te_ref, w_ref, ow_ref, cov_ref,
     newcov_ref, weight_ref,
     select, cov_hi, cov_lo, order, jrow_send, jcol_send, e_send, jr_recv, jc_recv, e_recv, e_all,
-    jr_all, jc_all, w_send, w_recv, art, turned, act,
-    s_send, s_x, s_y, s_all,
-    send, recv, jc_y, jc_x, act_y, s_z, s_g, turn_send, turn_recv,
+    jr_all, jc_all, w_send, w_recv, art, act,
+    s_send, s_recv, s_rows, s_all,
+    send, recv, jc_y, jc_x, act_in, act_x,
 ):
     r = lax.axis_index("row")
     c = lax.axis_index("col")
@@ -109,13 +109,21 @@
         pl.semaphore_signal(barrier, inc=1, device_id={"col": col_peer(j)}, device_id_type=MESH)
 
     across = lax.div(r, 2)
-    for h in range(2):
-
-        @pl.when(2 * c + h != r)
-        def _():
-            pl.semaphore_signal(
-                barrier, inc=1, device_id={"row": 2 * c + h, "col": across}, device_id_type=MESH
-            )
+    source = z * NX + x
+    takes = lax.div(x, 2) == k
+    half = lax.rem(x, 2)
+
+    @pl.when(takes)
+    def _():
+        @pl.loop(0, NC)
+        def _(p):
+            @pl.when((source != r) | (p != c))
+            def _():
+                pl.semaphore_signal(
+                    barrier, inc=1, device_id={"row": source, "col": p}, device_id_type=MESH
+                )
+
+    own_target = across == c
 
     block = 32
 
@@ -150,8 +158,7 @@
     to = lax.broadcasted_iota(jnp.int32, (512, 512), 1)
     order[...] = (to == lax.rem(at, NC) * NR + lax.div(at, NC)).astype(F32).astype(BF16)
 
-    mirror = lax.div(r, 2) == c
-    pl.semaphore_wait(barrier, NR - 1 + NC - 1 + 2 - mirror.astype(jnp.int32))
+    pl.semaphore_wait(barrier, NR - 1 + NC - 1 + NY - own_target.astype(jnp.int32))
 
     @pl.loop(1, NC)
     def _(j):
@@ -236,60 +243,63 @@
     own = jnp.sum(w_recv[...], axis=0)
     art[z, k] = own
 
-    for h in range(2):
-
-        @pl.when(2 * c + h != r)
-        def _():
-            pltpu.make_async_remote_copy(
-                src_ref=art.at[z, k, pl.ds(16 * h, 16)], dst_ref=turned.at[lax.rem(r, 2)],
-                send_sem=turn_send.at[h], recv_sem=turn_recv.at[lax.rem(r, 2)],
-                device_id={"row": 2 * c + h, "col": across}, device_id_type=MESH,
-            ).start()
-
-        @pl.when(2 * c + h == r)
-        def _():
-            turned[h] = own[16 * h : 16 * h + 16, :]
+    for j in (0,) + NEAR:
+        to_row = y_peer(j)
+        if j == 0:
+
+            @pl.when(jnp.logical_not(own_target))
+            def _():
+                push("act", art.at[z, k], act.at[half, c], act_in.at[c], row=to_row, col=across)
+
+            @pl.when(own_target)
+            def _():
+                act[half, c] = own
+
+        else:
+            push("act", art.at[z, k], act.at[half, c], act_in.at[c], row=to_row, col=across)
+    track("act", art.at[pl.ds(0, NY - 1), 0])
 
     s_part = dot3(own, jr, ROWS)
-    for n in range(NX):
-        s_send[n] = s_part[8 * n : 8 * n + 8, :]
-    for i in (1, 3, 2):
-        push("s_x", s_send.at[lax.rem(x + i, NX)], s_x.at[x], row=x_peer(i))
-    track("s_x", s_x.at[pl.ds(0, NX - 1)], s_x.at[pl.ds(0, NX - 1)])
-    s_x[x] = s_send[x]
+    for n in range(4):
+        s_send[:, n, :] = s_part[:, 128 * n : 128 * n + 128]
+
+    @pl.loop(1, NR)
+    def _(j):
+        p = row_peer(j)
+        push("s", s_send.at[lax.rem(p, NX) * NY + lax.div(p, NX)], s_recv.at[r], row=p)
+
+    track("s", s_send.at[pl.ds(0, NR - 1)], s_recv.at[pl.ds(0, NR - 1)])
+    s_recv[r] = s_send[x * NY + y]
 
     for j in NEAR:
         push("art_z", art.at[z, k], art.at[z, k], col=z_peer(j))
     track("art_z", art.at[pl.ds(0, NZ - 1), 0], art.at[pl.ds(0, NZ - 1), 0])
 
-    land("s_x")
-    s_y[y] = jnp.sum(s_x[...], axis=0)
-    for j in NEAR:
-        push("s_y", s_y.at[y], s_y.at[y], row=y_peer(j))
-    track("s_y", s_y.at[pl.ds(0, NY - 1)], s_y.at[pl.ds(0, NY - 1)])
-
-    for h in range(2):
-
-        @pl.when(2 * c + h != r)
-        def _():
-            settle(turned.at[h], turn_recv.at[h])
-            settle(turned.at[h], turn_send.at[h])
-
-    act[r] = jnp.concatenate([turned[0], turned[1]], axis=1)
-    for j in NEAR:
-        push("act_y", act.at[r], act.at[r], act_y.at[j], row=y_peer(j))
-    for i in (1, 3, 2):
-        push("act_x", act.at[r], act.at[r], row=x_peer(i))
-    track("act_y", act.at[pl.ds(0, NY - 1)])
-
-    land("s_y")
-    mine = c * NX + x
-    s_all[mine] = jnp.sum(s_y[...], axis=0)
-    for j in NEAR:
-        push("s_z", s_all.at[mine], s_all.at[mine], s_z.at[j], col=z_peer(j))
-    for i in (1, 3, 2):
-        push("s_g", s_all.at[mine], s_all.at[mine], s_g.at[0], row=x_peer(i))
-    track("s_z", s_all.at[pl.ds(0, NZ - 1)])
+    land("s")
+    spot = z * NY + y
+    s_rows[spot] = jnp.sum(s_recv[...], axis=0)
+
+    @pl.loop(1, NY * NZ)
+    def _(j):
+        to_row = lax.rem(y + lax.div(j, NZ), NY) * NX + x
+        to_col = lax.rem(z + lax.rem(j, NZ), NZ) * 2 + k
+        push("s_yz", s_rows.at[spot], s_rows.at[spot], row=to_row, col=to_col)
+
+    most = s_rows.at[pl.ds(0, NY * NZ - 1)]
+    track("s_yz", most, most)
+
+    @pl.when(takes)
+    def _():
+        for j in (0, 1, 7, 2, 6, 3, 5, 4):
+            for h in range(2):
+                p = lax.rem(z + j, NZ) * 2 + h
+
+                @pl.when((source != r) | (p != c))
+                def _():
+                    settle(act.at[half, p], act_in.at[p])
+
+                for i in (1, 3, 2):
+                    push("act_x", act.at[half, p], act.at[half, p], act_x.at[half], row=x_peer(i))
 
     land("art_z")
     push("art_p", art.at[:, k], art.at[:, k], col=partner)
@@ -301,22 +311,15 @@
 
     track("e", e_all.at[pl.ds(0, NR - 1)], e_all.at[pl.ds(0, NR - 1)])
 
-    for j in NEAR:
-        slot = z_peer(NZ - j) * NX + x
-        settle(s_all.at[slot], s_z.at[j])
-        for i in (1, 3, 2):
-            push("s_g", s_all.at[slot], s_all.at[slot], s_g.at[j], row=x_peer(i))
-        slot = y_peer(NY - j)
-        settle(act.at[slot], act_y.at[j])
-        for i in (1, 3, 2):
-            push("act_x", act.at[slot], act.at[slot], row=x_peer(i))
-    track("s_g", s_all.at[pl.ds(0, NX * NZ - NZ)])
-    track("act_x", act.at[pl.ds(0, NR - NY)], act.at[pl.ds(0, NR - NY)])
-    for j in (0,) + NEAR:
-        settle(s_all.at[pl.ds(0, NX - 1)], s_g.at[j])
-        group = pl.ds(z_peer(NZ - j) * NX, NX)
-        push("s_p", s_all.at[group], s_all.at[group], col=partner)
-    track("s_p", s_all.at[pl.ds(0, NX * NZ)], s_all.at[pl.ds(0, NX * NZ)])
+    land("s_yz")
+    for n in range(NZ):
+        s_all[n, k, x] = jnp.concatenate([s_rows[NY * n : NY * n + NY, i, :] for i in range(4)], axis=1)
+    for i in (1, 3, 2):
+        push("s_x", s_all.at[:, k, x], s_all.at[:, k, x], row=x_peer(i))
+    track("s_x", s_all.at[:, 0, pl.ds(0, NX - 1)], s_all.at[:, 0, pl.ds(0, NX - 1)])
+    land("s_x")
+    push("s_p", s_all.at[:, k], s_all.at[:, k], col=partner)
+    track("s_p", s_all.at[:, 0], s_all.at[:, 0])
     land("s_p")
 
     eye = at == to
@@ -342,15 +345,33 @@
     )
     column = jnp.sum(jnp.where(own_lane, picked, 0.0), axis=1, keepdims=True)
     delta = jnp.sum(gain * column, axis=0, keepdims=True)
-    half = lax.div(c, 8)
-    delta = jnp.where(half == 0, delta[:, :128], delta[:, 128:])
-    moved = w_ref[pl.ds(2 * r + half, 1), :] + delta
+    upper = lax.div(c, 8)
+    delta = jnp.where(upper == 0, delta[:, :128], delta[:, 128:])
+    moved = w_ref[pl.ds(2 * r + upper, 1), :] + delta
     moved = pltpu.roll(moved, 128 - 16 * lax.rem(c, 8), 1)
     weight_ref[...] = moved[:, :16]
 
-    land("act_x")
-    update = dot3(gain, act[...].reshape(512, 512), COLS)
-    newcov_ref[...] = (cov_ref[...] - update) * (1.0 / FORGET)
+    for h in range(2):
+
+        @pl.when(jnp.logical_not(takes & (half == h)))
+        def _():
+            settle(act.at[h], act_x.at[h])
+
+    gain = split(gain)
+    for h in range(2):
+        update = dot3(gain, act[h].reshape(512, 256), COLS)
+        columns = slice(256 * h, 256 * h + 256)
+        newcov_ref[:, columns] = (cov_ref[:, columns] - update) * (1.0 / FORGET)
+
+    @pl.when(jnp.logical_not(own_target))
+    def _():
+        settle(art.at[0, 0], send.at[GROUPS.index("act")])
+
+    @pl.when(takes)
+    def _():
+        for i in range(3):
+            settle(act.at[0], send.at[GROUPS.index("act_x")])
+
     drain()
 
 
@@ -367,10 +388,9 @@
         V((NR, 2, 128), F32), V((NC, 4, 128), F32), V((NC, 1, 128), F32), V((NR, 1, 128), F32),
         V((NZ, 2, NR, 256), F32), V((NR, NC, 512), F32),
         V((NY, 2, NR, 256), F32), V((NC, NR, 256), F32), V((NZ, 2, NR, 256), F32),
-        V((2, 16, 256), F32), V((NR, 16, 512), F32),
-        V((NX, 8, 512), F32), V((NX, 8, 512), F32), V((NY, 8, 512), F32), V((NC * NX, 8, 512), F32),
-        D((len(GROUPS),)), D((len(GROUPS),)), D((NY,)), D((NY,)), D((NY,)), D((NZ,)), D((NZ,)),
-        D((2,)), D((2,)),
+        V((2, NC, NR, 256), F32),
+        V((NR, 4, 128), F32), V((NR, 4, 128), F32), V((NZ * NY, 4, 128), F32), V((NZ, 2, NX, 8, 512), F32),
+        D((len(GROUPS),)), D((len(GROUPS),)), D((NY,)), D((NY,)), D((NC,)), D((2,)),
     ]
     new_cov, weight = pl.pallas_call(
         kernel,

time: 95.7 us -> 96.2 us (level)
  no operation moved by 1% of the time
where the time goes in v3:
time: 96.2 us; the launch traced here: 96 us
  Pallas kernels  91.6 us (95%)
  local copies, waits for them, and re-layouts  3.04 us (3%)
  between operations  1.3 us (1%)
    pallas_call x1, Pallas kernels, on_device(): pl.pallas_call(kernel, out_shape=(jax.ShapeDtypeStruct((256, 512), F32),...  91.6 us
    unnamed x4, local copies, waits for them, and re-layouts  3.04 us

profile of v3, /device:TPU:1, one launch (start us, length us, event | category | flops | bytes accessed | tf_op | source)
XLA Modules:
  0.0 96.0 jit_solution(10469672585242547748)
XLA Ops:
  1.3 91.6 %shard_map.113 = (f32[256,512]{1,0:T(8,128)}, f32[1,16]{1,0:T(1,128)}) custom-call(s32[1,256]{1,0:T(1,128)} %types_ref.1, s32[32,256]{1,0:T(8,128)} %bitcast.10, f32[32,256]{1,0:T(8,128)} %bitcast.11, f32[64,256]{1,0:T(8,128)} %bitcast.9, f32[1,256]{1,0:T(1,128)} %fw_ref.1, f32[1,1]{1,0:T(1,128)} %bitcast.8.tgt_ref, f32[4,64]{1,0:T(4,128)} %te_ref.1, ...), custom_call_target="tpu_custom_call" | custom-call | tf_op jit(solution)/shard_map/pallas_call | solution.py:395
  92.9 0.0 copy-start
  92.9 0.7 copy-done
  93.6 0.5 copy.15
  94.1 1.9 %copy.16 = f32[256,512]{1,0:T(8,128)} copy(f32[256,512]{1,0:T(8,128)} %get-tuple-element.9) | data formatting | bytes 1048576
Async XLA Ops:
  92.9 0.7 copy-start

commit v4 on v3

--- a/solution.py
+++ b/solution.py
@@ -44,11 +44,11 @@
 
 def kernel(
     types_ref, nbr_ref, sw_ref, env_ref, fw_ref, tgt_ref, te_ref, w_ref, ow_ref, cov_ref,
-    newcov_ref, weight_ref,
+    gain_ref, act, weight_ref,
     select, cov_hi, cov_lo, order, jrow_send, jcol_send, e_send, jr_recv, jc_recv, e_recv, e_all,
-    jr_all, jc_all, w_send, w_recv, art, act,
+    jr_all, jc_all, w_send, w_recv, art,
     s_send, s_recv, s_rows, s_all,
-    send, recv, jc_y, jc_x, act_in, act_x,
+    send, recv, jc_y, jc_x, act_in, act_x, s_g,
 ):
     r = lax.axis_index("row")
     c = lax.axis_index("col")
@@ -243,6 +243,18 @@
     own = jnp.sum(w_recv[...], axis=0)
     art[z, k] = own
 
+    s_part = dot3(own, jr, ROWS)
+    for n in range(4):
+        s_send[:, n, :] = s_part[:, 128 * n : 128 * n + 128]
+
+    @pl.loop(1, NR)
+    def _(j):
+        p = row_peer(j)
+        push("s", s_send.at[lax.rem(p, NX) * NY + lax.div(p, NX)], s_recv.at[r], row=p)
+
+    track("s", s_send.at[pl.ds(0, NR - 1)], s_recv.at[pl.ds(0, NR - 1)])
+    s_recv[r] = s_send[x * NY + y]
+
     for j in (0,) + NEAR:
         to_row = y_peer(j)
         if j == 0:
@@ -259,34 +271,22 @@
             push("act", art.at[z, k], act.at[half, c], act_in.at[c], row=to_row, col=across)
     track("act", art.at[pl.ds(0, NY - 1), 0])
 
-    s_part = dot3(own, jr, ROWS)
-    for n in range(4):
-        s_send[:, n, :] = s_part[:, 128 * n : 128 * n + 128]
-
-    @pl.loop(1, NR)
-    def _(j):
-        p = row_peer(j)
-        push("s", s_send.at[lax.rem(p, NX) * NY + lax.div(p, NX)], s_recv.at[r], row=p)
-
-    track("s", s_send.at[pl.ds(0, NR - 1)], s_recv.at[pl.ds(0, NR - 1)])
-    s_recv[r] = s_send[x * NY + y]
+    land("s")
+    spot = z * NY + y
+    s_rows[spot] = jnp.sum(s_recv[...], axis=0)
+
+    @pl.loop(1, NY * NZ)
+    def _(j):
+        to_row = lax.rem(y + lax.div(j, NZ), NY) * NX + x
+        to_col = lax.rem(z + lax.rem(j, NZ), NZ) * 2 + k
+        push("s_yz", s_rows.at[spot], s_rows.at[spot], row=to_row, col=to_col)
+
+    most = s_rows.at[pl.ds(0, NY * NZ - 1)]
+    track("s_yz", most, most)
 
     for j in NEAR:
         push("art_z", art.at[z, k], art.at[z, k], col=z_peer(j))
     track("art_z", art.at[pl.ds(0, NZ - 1), 0], art.at[pl.ds(0, NZ - 1), 0])
-
-    land("s")
-    spot = z * NY + y
-    s_rows[spot] = jnp.sum(s_recv[...], axis=0)
-
-    @pl.loop(1, NY * NZ)
-    def _(j):
-        to_row = lax.rem(y + lax.div(j, NZ), NY) * NX + x
-        to_col = lax.rem(z + lax.rem(j, NZ), NZ) * 2 + k
-        push("s_yz", s_rows.at[spot], s_rows.at[spot], row=to_row, col=to_col)
-
-    most = s_rows.at[pl.ds(0, NY * NZ - 1)]
-    track("s_yz", most, most)
 
     @pl.when(takes)
     def _():
@@ -301,10 +301,6 @@
                 for i in (1, 3, 2):
                     push("act_x", act.at[half, p], act.at[half, p], act_x.at[half], row=x_peer(i))
 
-    land("art_z")
-    push("art_p", art.at[:, k], art.at[:, k], col=partner)
-    track("art_p", art.at[:, 0], art.at[:, 0])
-
     @pl.loop(1, NR)
     def _(j):
         push("e", e_all.at[r], e_all.at[r], row=row_peer(j))
@@ -315,10 +311,16 @@
     for n in range(NZ):
         s_all[n, k, x] = jnp.concatenate([s_rows[NY * n : NY * n + NY, i, :] for i in range(4)], axis=1)
     for i in (1, 3, 2):
-        push("s_x", s_all.at[:, k, x], s_all.at[:, k, x], row=x_peer(i))
-    track("s_x", s_all.at[:, 0, pl.ds(0, NX - 1)], s_all.at[:, 0, pl.ds(0, NX - 1)])
-    land("s_x")
-    push("s_p", s_all.at[:, k], s_all.at[:, k], col=partner)
+        push("s_x", s_all.at[:, k, x], s_all.at[:, k, x], s_g.at[i], row=x_peer(i))
+    track("s_x", s_all.at[:, 0, pl.ds(0, NX - 1)])
+    push("s_p", s_all.at[:, k, x], s_all.at[:, k, x], col=partner)
+    land("art_z")
+    push("art_p", art.at[:, k], art.at[:, k], col=partner)
+    track("art_p", art.at[:, 0], art.at[:, 0])
+    for i in (1, 3, 2):
+        origin = lax.rem(x + NX - i, NX)
+        settle(s_all.at[:, k, origin], s_g.at[i])
+        push("s_p", s_all.at[:, k, origin], s_all.at[:, k, origin], col=partner)
     track("s_p", s_all.at[:, 0], s_all.at[:, 0])
     land("s_p")
 
@@ -328,10 +330,12 @@
     land("art_p")
     power = split(jnp.where(eye, 1.0, 0.0) - innovation / bound)
     gain = art[...].reshape(512, 256) / bound
-    for step in range(4):
+    gain = gain + dot3(power, gain, NORMAL)
+    for step in range(2):
+        power = split(dot3(power, power, NORMAL))
         gain = gain + dot3(power, gain, NORMAL)
-        if step < 3:
-            power = split(dot3(power, power, NORMAL))
+    gain = gain + dot3(power, dot3(power, gain, NORMAL), NORMAL)
+    gain_ref[...] = gain
 
     land("e")
     spread = (
@@ -357,12 +361,6 @@
         def _():
             settle(act.at[h], act_x.at[h])
 
-    gain = split(gain)
-    for h in range(2):
-        update = dot3(gain, act[h].reshape(512, 256), COLS)
-        columns = slice(256 * h, 256 * h + 256)
-        newcov_ref[:, columns] = (cov_ref[:, columns] - update) * (1.0 / FORGET)
-
     @pl.when(jnp.logical_not(own_target))
     def _():
         settle(art.at[0, 0], send.at[GROUPS.index("act")])
@@ -373,6 +371,12 @@
             settle(act.at[0], send.at[GROUPS.index("act_x")])
 
     drain()
+
+
+def finish(gain_ref, act_ref, cov_ref, weight_ref, newcov_ref, new_weight_ref):
+    update = dot3(gain_ref[...], act_ref[0], COLS)
+    newcov_ref[...] = (cov_ref[...] - update) * (1.0 / FORGET)
+    new_weight_ref[...] = weight_ref[...]
 
 
 def on_device(
@@ -388,18 +392,18 @@
         V((NR, 2, 128), F32), V((NC, 4, 128), F32), V((NC, 1, 128), F32), V((NR, 1, 128), F32),
         V((NZ, 2, NR, 256), F32), V((NR, NC, 512), F32),
         V((NY, 2, NR, 256), F32), V((NC, NR, 256), F32), V((NZ, 2, NR, 256), F32),
-        V((2, NC, NR, 256), F32),
         V((NR, 4, 128), F32), V((NR, 4, 128), F32), V((NZ * NY, 4, 128), F32), V((NZ, 2, NX, 8, 512), F32),
-        D((len(GROUPS),)), D((len(GROUPS),)), D((NY,)), D((NY,)), D((NC,)), D((2,)),
+        D((len(GROUPS),)), D((len(GROUPS),)), D((NY,)), D((NY,)), D((NC,)), D((2,)), D((NX,)),
     ]
-    new_cov, weight = pl.pallas_call(
+    gain, act, weight = pl.pallas_call(
         kernel,
         out_shape=(
-            jax.ShapeDtypeStruct((256, 512), F32),
+            jax.ShapeDtypeStruct((512, 256), F32),
+            jax.ShapeDtypeStruct((2, NC, NR, 256), F32),
             jax.ShapeDtypeStruct((1, 16), F32),
         ),
         in_specs=[vmem] * 10,
-        out_specs=(vmem, vmem),
+        out_specs=(vmem, vmem, vmem),
         scratch_shapes=scratch,
         compiler_params=pltpu.CompilerParams(
             collective_id=0, has_side_effects=True, vmem_limit_bytes=60 * 1024 * 1024
@@ -408,7 +412,25 @@
         atom_types, neighbor_ids[0], switching[0], environment[0].T, force_weights,
         targets.reshape(1, 1), type_embed, layer_weight, out_weight.reshape(1, 128), covariance,
     )
-    return (weight.reshape(16), new_cov)
+    new_cov, new_weight = pl.pallas_call(
+        finish,
+        grid=(2,),
+        out_shape=(
+            jax.ShapeDtypeStruct((256, 512), F32),
+            jax.ShapeDtypeStruct((1, 16), F32),
+        ),
+        in_specs=[
+            pl.BlockSpec((512, 256), lambda h: (0, 0)),
+            pl.BlockSpec((1, 512, 256), lambda h: (h, 0, 0)),
+            pl.BlockSpec((256, 256), lambda h: (0, h)),
+            pl.BlockSpec((1, 16), lambda h: (0, 0)),
+        ],
+        out_specs=(
+            pl.BlockSpec((256, 256), lambda h: (0, h)),
+            pl.BlockSpec((1, 16), lambda h: (0, 0)),
+        ),
+    )(gain, act.reshape(2, 512, 256), covariance, weight)
+    return (new_weight.reshape(16), new_cov)
 
 
 def solution(mesh):

time: 96.2 us -> 88.8 us (0.923)
  Pallas kernels: 91.6 us -> 87.2 us
  local copies, waits for them, and re-layouts: 3.04 us -> 0 us
    pallas_call x1 -> x2, Pallas kernels: 91.6 us -> 87.2 us  [the longest x1 84.3 us: on_device(): pl.pallas_call(kernel, out_shape=(jax.ShapeDtypeStruct((512, 256), F32),...]
    unnamed x4 -> x0, local copies, waits for them, and re-layouts: 3.04 us -> none
where the time goes in v4:
time: 88.8 us; the launch traced here: 88.5 us
  Pallas kernels  87.2 us (98%)
  between operations  1.29 us (1%)
    pallas_call x1, Pallas kernels, on_device(): pl.pallas_call(kernel, out_shape=(jax.ShapeDtypeStruct((512, 256), F32),...  84.3 us
    pallas_call x1, Pallas kernels, on_device(): pl.pallas_call(finish, grid=(2,), out_shape=(jax.ShapeDtypeStruct((256, 5...  2.91 us

profile of v4, /device:TPU:1, one launch (start us, length us, event | category | flops | bytes accessed | tf_op | source)
XLA Modules:
  0.0 88.5 jit_solution(5786383312021079435)
XLA Ops:
  1.3 84.3 %shard_map.113 = (f32[512,256]{1,0:T(8,128)}, f32[2,16,32,256]{3,2,1,0:T(8,128)}, f32[1,16]{1,0:T(1,128)}) custom-call(s32[1,256]{1,0:T(1,128)} %types_ref.1, s32[32,256]{1,0:T(8,128)} %bitcast.12, f32[32,256]{1,0:T(8,128)} %bitcast.13, f32[64,256]{1,0:T(8,128)} %bitcast.11, f32[1,256]{1,0:T(1,128)} %fw_ref.1, f32[1,1]{1,0:T(1,128)} %bitcast.9.tgt_ref, ...), custom_call_target="tpu_custom_call" | custom-call | tf_op jit(solution)/shard_map/pallas_call | solution.py:398
  85.6 2.9 %shard_map.114 = (f32[256,512]{1,0:T(8,128)}, f32[1,16]{1,0:T(1,128)}) custom-call(f32[512,256]{1,0:T(8,128)} %get-tuple-element.7.gain_ref, f32[2,512,256]{2,1,0:T(8,128)} %bitcast.10, f32[256,512]{1,0:T(8,128)} %cov_ref.3, f32[1,16]{1,0:T(1,128)} %get-tuple-element.9.weight_ref), custom_call_target="tpu_custom_call" | custom-call | tf_op jit(solution)/shard_map/pallas_call | solution.py:415

commit v5 on v4

--- a/solution.py
+++ b/solution.py
@@ -1,4 +1,5 @@
 import functools
+import itertools
 import math
 
 import jax
@@ -15,6 +16,13 @@
 NX, NY, NZ = 4, 8, 8
 NR, NC = 32, 16
 NEAR = (1, 7, 2, 6, 3, 5, 4)
+
+
+def far_first(*sizes):
+    spots = [o for o in itertools.product(*map(range, sizes)) if any(o)]
+    return sorted(spots, key=lambda o: -sum(min(d, n - d) for d, n in zip(o, sizes)))
+
+
 GROUPS = (
     "jcol", "jrow", "err", "jc_y", "jc_x", "jr_z", "jr_p", "e", "w", "art_z", "art_p",
     "s", "s_yz", "s_x", "s_p", "act", "act_x",
@@ -160,9 +168,11 @@
 
     pl.semaphore_wait(barrier, NR - 1 + NC - 1 + NY - own_target.astype(jnp.int32))
 
-    @pl.loop(1, NC)
-    def _(j):
-        p = col_peer(j)
+    zs = [lax.rem(z + d, NZ) * 2 for d in range(NZ)]
+    ys = [lax.rem(y + d, NY) for d in range(NY)]
+    xs = [lax.rem(x + d, NX) for d in range(NX)]
+    for dz, dk in far_first(NZ, 2):
+        p = zs[dz] + (k if dk == 0 else 1 - k)
         push("jcol", jcol_send.at[p], jc_recv.at[c], col=p)
 
     @pl.loop(1, NR)
@@ -247,10 +257,8 @@
     for n in range(4):
         s_send[:, n, :] = s_part[:, 128 * n : 128 * n + 128]
 
-    @pl.loop(1, NR)
-    def _(j):
-        p = row_peer(j)
-        push("s", s_send.at[lax.rem(p, NX) * NY + lax.div(p, NX)], s_recv.at[r], row=p)
+    for dy, dx in far_first(NY, NX):
+        push("s", s_send.at[xs[dx] * NY + ys[dy]], s_recv.at[r], row=ys[dy] * NX + xs[dx])
 
     track("s", s_send.at[pl.ds(0, NR - 1)], s_recv.at[pl.ds(0, NR - 1)])
     s_recv[r] = s_send[x * NY + y]
@@ -275,11 +283,8 @@
     spot = z * NY + y
     s_rows[spot] = jnp.sum(s_recv[...], axis=0)
 
-    @pl.loop(1, NY * NZ)
-    def _(j):
-        to_row = lax.rem(y + lax.div(j, NZ), NY) * NX + x
-        to_col = lax.rem(z + lax.rem(j, NZ), NZ) * 2 + k
-        push("s_yz", s_rows.at[spot], s_rows.at[spot], row=to_row, col=to_col)
+    for dy, dz in far_first(NY, NZ):
+        push("s_yz", s_rows.at[spot], s_rows.at[spot], row=ys[dy] * NX + x, col=zs[dz] + k)
 
     most = s_rows.at[pl.ds(0, NY * NZ - 1)]
     track("s_yz", most, most)
@@ -322,20 +327,6 @@
         settle(s_all.at[:, k, origin], s_g.at[i])
         push("s_p", s_all.at[:, k, origin], s_all.at[:, k, origin], col=partner)
     track("s_p", s_all.at[:, 0], s_all.at[:, 0])
-    land("s_p")
-
-    eye = at == to
-    innovation = s_all[...].reshape(512, 512) + jnp.where(eye, FORGET, 0.0)
-    bound = jnp.max(jnp.sum(jnp.abs(innovation), axis=0, keepdims=True), axis=1, keepdims=True)
-    land("art_p")
-    power = split(jnp.where(eye, 1.0, 0.0) - innovation / bound)
-    gain = art[...].reshape(512, 256) / bound
-    gain = gain + dot3(power, gain, NORMAL)
-    for step in range(2):
-        power = split(dot3(power, power, NORMAL))
-        gain = gain + dot3(power, gain, NORMAL)
-    gain = gain + dot3(power, dot3(power, gain, NORMAL), NORMAL)
-    gain_ref[...] = gain
 
     land("e")
     spread = (
@@ -347,8 +338,29 @@
     own_lane = lax.broadcasted_iota(jnp.int32, (512, 128), 1) == lax.rem(
         lax.broadcasted_iota(jnp.int32, (512, 128), 0), NC
     )
-    column = jnp.sum(jnp.where(own_lane, picked, 0.0), axis=1, keepdims=True)
-    delta = jnp.sum(gain * column, axis=0, keepdims=True)
+    errors = dot3(jnp.ones((8, 128), F32), jnp.where(own_lane, picked, 0.0), ROWS)
+    land("art_p")
+    products = art[...].reshape(512, 256).T
+    land("s_p")
+
+    eye = at == to
+    innovation = s_all[...].reshape(512, 512) + jnp.where(eye, FORGET, 0.0)
+    bound = jnp.max(jnp.sum(jnp.abs(innovation), axis=0, keepdims=True), axis=1, keepdims=True)
+    ph, pw = split(jnp.where(eye, 1.0, 0.0) - innovation / bound)
+    gain = products / bound
+    for step in range(2):
+        gh, gl = split(gain)
+        first = mm(jnp.concatenate([ph, gh, gl], axis=0), ph, NORMAL)
+        second = mm(jnp.concatenate([ph, gh], axis=0), pw, NORMAL)
+        mixed = second[:512]
+        gain = gain + (first[512:768] + (first[768:] + second[512:]))
+        ph, pw = split(first[:512] + (mixed + mixed.T))
+    power = (ph, pw)
+    gain = gain + dot3(gain, power, NORMAL)
+    gain = gain + dot3(dot3(gain, power, NORMAL), power, NORMAL)
+    gain_ref[...] = gain
+
+    delta = dot3(errors, gain, ROWS)[:1]
     upper = lax.div(c, 8)
     delta = jnp.where(upper == 0, delta[:, :128], delta[:, 128:])
     moved = w_ref[pl.ds(2 * r + upper, 1), :] + delta
@@ -374,7 +386,7 @@
 
 
 def finish(gain_ref, act_ref, cov_ref, weight_ref, newcov_ref, new_weight_ref):
-    update = dot3(gain_ref[...], act_ref[0], COLS)
+    update = dot3(gain_ref[...], act_ref[0], NORMAL)
     newcov_ref[...] = (cov_ref[...] - update) * (1.0 / FORGET)
     new_weight_ref[...] = weight_ref[...]
 
@@ -398,7 +410,7 @@
     gain, act, weight = pl.pallas_call(
         kernel,
         out_shape=(
-            jax.ShapeDtypeStruct((512, 256), F32),
+            jax.ShapeDtypeStruct((256, 512), F32),
             jax.ShapeDtypeStruct((2, NC, NR, 256), F32),
             jax.ShapeDtypeStruct((1, 16), F32),
         ),
@@ -420,7 +432,7 @@
             jax.ShapeDtypeStruct((1, 16), F32),
         ),
         in_specs=[
-            pl.BlockSpec((512, 256), lambda h: (0, 0)),
+            pl.BlockSpec((256, 512), lambda h: (0, 0)),
             pl.BlockSpec((1, 512, 256), lambda h: (h, 0, 0)),
             pl.BlockSpec((256, 256), lambda h: (0, h)),
             pl.BlockSpec((1, 16), lambda h: (0, 0)),

time: 88.8 us -> 85.9 us (0.967)
  Pallas kernels: 87.2 us -> 84.3 us
    pallas_call x1, Pallas kernels: 84.3 us -> 81.5 us  [on_device(): pl.pallas_call(kernel, out_shape=(jax.ShapeDtypeStruct((256, 512), F32),...]
where the time goes in v5:
time: 85.9 us; the launch traced here: 85.6 us
  Pallas kernels  84.3 us (98%)
  between operations  1.29 us (2%)
    pallas_call x1, Pallas kernels, on_device(): pl.pallas_call(kernel, out_shape=(jax.ShapeDtypeStruct((256, 512), F32),...  81.5 us
    pallas_call x1, Pallas kernels, on_device(): pl.pallas_call(finish, grid=(2,), out_shape=(jax.ShapeDtypeStruct((256, 5...  2.81 us

profile of v5, /device:TPU:1, one launch (start us, length us, event | category | flops | bytes accessed | tf_op | source)
XLA Modules:
  0.0 85.6 jit_solution(16077202301675088535)
XLA Ops:
  1.3 81.5 %shard_map.113 = (f32[256,512]{1,0:T(8,128)}, f32[2,16,32,256]{3,2,1,0:T(8,128)}, f32[1,16]{1,0:T(1,128)}) custom-call(s32[1,256]{1,0:T(1,128)} %types_ref.1, s32[32,256]{1,0:T(8,128)} %bitcast.12, f32[32,256]{1,0:T(8,128)} %bitcast.13, f32[64,256]{1,0:T(8,128)} %bitcast.11, f32[1,256]{1,0:T(1,128)} %fw_ref.1, f32[1,1]{1,0:T(1,128)} %bitcast.9.tgt_ref, ...), custom_call_target="tpu_custom_call" | custom-call | tf_op jit(solution)/shard_map/pallas_call | solution.py:410
  82.8 2.8 %shard_map.114 = (f32[256,512]{1,0:T(8,128)}, f32[1,16]{1,0:T(1,128)}) custom-call(f32[256,512]{1,0:T(8,128)} %get-tuple-element.7.gain_ref, f32[2,512,256]{2,1,0:T(8,128)} %bitcast.10, f32[256,512]{1,0:T(8,128)} %cov_ref.3, f32[1,16]{1,0:T(1,128)} %get-tuple-element.9.weight_ref), custom_call_target="tpu_custom_call" | custom-call | tf_op jit(solution)/shard_map/pallas_call | solution.py:427

commit v6 on v5

--- a/solution.py
+++ b/solution.py
@@ -56,7 +56,7 @@
     select, cov_hi, cov_lo, order, jrow_send, jcol_send, e_send, jr_recv, jc_recv, e_recv, e_all,
     jr_all, jc_all, w_send, w_recv, art,
     s_send, s_recv, s_rows, s_all,
-    send, recv, jc_y, jc_x, act_in, act_x, s_g,
+    send, recv, jc_y, jc_x, act_in, act_x, s_z, s_g,
 ):
     r = lax.axis_index("row")
     c = lax.axis_index("col")
@@ -284,10 +284,9 @@
     s_rows[spot] = jnp.sum(s_recv[...], axis=0)
 
     for dy, dz in far_first(NY, NZ):
-        push("s_yz", s_rows.at[spot], s_rows.at[spot], row=ys[dy] * NX + x, col=zs[dz] + k)
-
-    most = s_rows.at[pl.ds(0, NY * NZ - 1)]
-    track("s_yz", most, most)
+        push("s_yz", s_rows.at[spot], s_rows.at[spot], s_z.at[dz], row=ys[dy] * NX + x, col=zs[dz] + k)
+
+    track("s_yz", s_rows.at[pl.ds(0, NY * NZ - 1)])
 
     for j in NEAR:
         push("art_z", art.at[z, k], art.at[z, k], col=z_peer(j))
@@ -312,11 +311,13 @@
 
     track("e", e_all.at[pl.ds(0, NR - 1)], e_all.at[pl.ds(0, NR - 1)])
 
-    land("s_yz")
-    for n in range(NZ):
-        s_all[n, k, x] = jnp.concatenate([s_rows[NY * n : NY * n + NY, i, :] for i in range(4)], axis=1)
-    for i in (1, 3, 2):
-        push("s_x", s_all.at[:, k, x], s_all.at[:, k, x], s_g.at[i], row=x_peer(i))
+    for dz in (0,) + NEAR:
+        n = lax.rem(z + NZ - dz, NZ)
+        settle(s_rows.at[pl.ds(0, NY if dz else NY - 1)], s_z.at[dz])
+        rows = s_rows[pl.ds(n * NY, NY)]
+        s_all[n, k, x] = jnp.concatenate([rows[:, i, :] for i in range(4)], axis=1)
+        for i in (1, 3, 2):
+            push("s_x", s_all.at[n, k, x], s_all.at[n, k, x], s_g.at[i], row=x_peer(i))
     track("s_x", s_all.at[:, 0, pl.ds(0, NX - 1)])
     push("s_p", s_all.at[:, k, x], s_all.at[:, k, x], col=partner)
     land("art_z")
@@ -405,7 +406,7 @@
         V((NZ, 2, NR, 256), F32), V((NR, NC, 512), F32),
         V((NY, 2, NR, 256), F32), V((NC, NR, 256), F32), V((NZ, 2, NR, 256), F32),
         V((NR, 4, 128), F32), V((NR, 4, 128), F32), V((NZ * NY, 4, 128), F32), V((NZ, 2, NX, 8, 512), F32),
-        D((len(GROUPS),)), D((len(GROUPS),)), D((NY,)), D((NY,)), D((NC,)), D((2,)), D((NX,)),
+        D((len(GROUPS),)), D((len(GROUPS),)), D((NY,)), D((NY,)), D((NC,)), D((2,)), D((NZ,)), D((NX,)),
     ]
     gain, act, weight = pl.pallas_call(
         kernel,

time: 85.9 us -> 86.9 us (1.012)
  Pallas kernels: 84.3 us -> 85.4 us
    pallas_call x1, Pallas kernels: 81.5 us -> 82.6 us  [on_device(): pl.pallas_call(kernel, out_shape=(jax.ShapeDtypeStruct((256, 512), F32),...]
where the time goes in v6:
time: 86.9 us; the launch traced here: 86.7 us
  Pallas kernels  85.4 us (98%)
  between operations  1.29 us (1%)
    pallas_call x1, Pallas kernels, on_device(): pl.pallas_call(kernel, out_shape=(jax.ShapeDtypeStruct((256, 512), F32),...  82.6 us
    pallas_call x1, Pallas kernels, on_device(): pl.pallas_call(finish, grid=(2,), out_shape=(jax.ShapeDtypeStruct((256, 5...  2.81 us

profile of v6, /device:TPU:1, one launch (start us, length us, event | category | flops | bytes accessed | tf_op | source)
XLA Modules:
  0.0 86.7 jit_solution(8574467387027598171)
XLA Ops:
  1.3 82.6 %shard_map.113 = (f32[256,512]{1,0:T(8,128)}, f32[2,16,32,256]{3,2,1,0:T(8,128)}, f32[1,16]{1,0:T(1,128)}) custom-call(s32[1,256]{1,0:T(1,128)} %types_ref.1, s32[32,256]{1,0:T(8,128)} %bitcast.12, f32[32,256]{1,0:T(8,128)} %bitcast.13, f32[64,256]{1,0:T(8,128)} %bitcast.11, f32[1,256]{1,0:T(1,128)} %fw_ref.1, f32[1,1]{1,0:T(1,128)} %bitcast.9.tgt_ref, ...), custom_call_target="tpu_custom_call" | custom-call | tf_op jit(solution)/shard_map/pallas_call | solution.py:411
  83.9 2.8 %shard_map.114 = (f32[256,512]{1,0:T(8,128)}, f32[1,16]{1,0:T(1,128)}) custom-call(f32[256,512]{1,0:T(8,128)} %get-tuple-element.7.gain_ref, f32[2,512,256]{2,1,0:T(8,128)} %bitcast.10, f32[256,512]{1,0:T(8,128)} %cov_ref.3, f32[1,16]{1,0:T(1,128)} %get-tuple-element.9.weight_ref), custom_call_target="tpu_custom_call" | custom-call | tf_op jit(solution)/shard_map/pallas_call | solution.py:428

commit v7 on v5

--- a/solution.py
+++ b/solution.py
@@ -386,7 +386,7 @@
 
 
 def finish(gain_ref, act_ref, cov_ref, weight_ref, newcov_ref, new_weight_ref):
-    update = dot3(gain_ref[...], act_ref[0], NORMAL)
+    update = dot3(gain_ref[...], act_ref[pl.program_id(0)], NORMAL)
     newcov_ref[...] = (cov_ref[...] - update) * (1.0 / FORGET)
     new_weight_ref[...] = weight_ref[...]
 
@@ -410,8 +410,8 @@
     gain, act, weight = pl.pallas_call(
         kernel,
         out_shape=(
-            jax.ShapeDtypeStruct((256, 512), F32),
-            jax.ShapeDtypeStruct((2, NC, NR, 256), F32),
+            V((256, 512), F32),
+            V((2, NC, NR, 256), F32),
             jax.ShapeDtypeStruct((1, 16), F32),
         ),
         in_specs=[vmem] * 10,
@@ -424,6 +424,7 @@
         atom_types, neighbor_ids[0], switching[0], environment[0].T, force_weights,
         targets.reshape(1, 1), type_embed, layer_weight, out_weight.reshape(1, 128), covariance,
     )
+    keep = functools.partial(pltpu.with_memory_space_constraint, memory_space=pltpu.VMEM)
     new_cov, new_weight = pl.pallas_call(
         finish,
         grid=(2,),
@@ -432,8 +433,8 @@
             jax.ShapeDtypeStruct((1, 16), F32),
         ),
         in_specs=[
-            pl.BlockSpec((256, 512), lambda h: (0, 0)),
-            pl.BlockSpec((1, 512, 256), lambda h: (h, 0, 0)),
+            vmem,
+            vmem,
             pl.BlockSpec((256, 256), lambda h: (0, h)),
             pl.BlockSpec((1, 16), lambda h: (0, 0)),
         ],
@@ -441,7 +442,7 @@
             pl.BlockSpec((256, 256), lambda h: (0, h)),
             pl.BlockSpec((1, 16), lambda h: (0, 0)),
         ),
-    )(gain, act.reshape(2, 512, 256), covariance, weight)
+    )(keep(gain), keep(act.reshape(2, 512, 256)), covariance, weight)
     return (new_weight.reshape(16), new_cov)
 
 

time: 85.9 us -> 84.9 us (0.988)
  Pallas kernels: 84.3 us -> 83.3 us
where the time goes in v7:
time: 84.9 us; the launch traced here: 84.6 us
  Pallas kernels  83.3 us (98%)
  between operations  1.29 us (2%)
    pallas_call x1, Pallas kernels, on_device(): pl.pallas_call(kernel, out_shape=(V((256, 512), F32), V((2, NC, NR, 256),...  80.8 us
    pallas_call x1, Pallas kernels, on_device(): pl.pallas_call(finish, grid=(2,), out_shape=(jax.ShapeDtypeStruct((256, 5...  2.46 us

profile of v7, /device:TPU:1, one launch (start us, length us, event | category | flops | bytes accessed | tf_op | source)
XLA Modules:
  0.0 84.6 jit_solution(17559515481319714037)
XLA Ops:
  1.3 80.8 %shard_map.113 = (f32[256,512]{1,0:T(8,128)S(1)}, f32[2,16,32,256]{3,2,1,0:T(8,128)S(1)}, f32[1,16]{1,0:T(1,128)}) custom-call(s32[1,256]{1,0:T(1,128)} %types_ref.1, s32[32,256]{1,0:T(8,128)} %bitcast.12, f32[32,256]{1,0:T(8,128)} %bitcast.13, f32[64,256]{1,0:T(8,128)} %bitcast.11, f32[1,256]{1,0:T(1,128)} %fw_ref.1, f32[1,1]{1,0:T(1,128)} %bitcast.9.tgt_ref, ...), custom_call_target="tpu_custom_call" | custom-call | tf_op jit(solution)/shard_map/pallas_call | solution.py:410
  82.1 2.5 %shard_map.114 = (f32[256,512]{1,0:T(8,128)}, f32[1,16]{1,0:T(1,128)}) custom-call(f32[256,512]{1,0:T(8,128)S(1)} %get-tuple-element.7.gain_ref, f32[2,512,256]{2,1,0:T(8,128)S(1)} %bitcast.10, f32[256,512]{1,0:T(8,128)} %cov_ref.3, f32[1,16]{1,0:T(1,128)} %get-tuple-element.9.weight_ref), custom_call_target="tpu_custom_call" | custom-call | tf_op jit(solution)/shard_map/pallas_call | solution.py:428
